TPU v7x, 256 devices: a whole 4x4x8 slice. The times are simulated.
256 devices in a mesh: row: 64 (over x, z, core), col: 4 (over y).
Axes of the slice: x: 4, y: 4, z: 8, core: 2. Of those that a mesh axis runs over, the one named last changes fastest.
Arguments:
- input_picture: bfloat16 [1024, 512, 256], P('row', 'col'), may hold values from -6 to 6
- spatial_taps_first: bfloat16 [2, 49, 256], replicated, may hold values from -0.875 to 0.875
- widening_matrix_first: bfloat16 [2, 256, 1024], replicated, may hold values from -0.375 to 0.375
- narrowing_matrix_first: bfloat16 [2, 1024, 256], replicated, may hold values from -0.1875 to 0.1875
- stride_kernel_matrix: bfloat16 [1024, 512], replicated, may hold values from -0.1875 to 0.1875
- spatial_taps_second: bfloat16 [2, 49, 512], replicated, may hold values from -0.875 to 0.875
- widening_matrix_second: bfloat16 [2, 512, 2048], replicated, may hold values from -0.25 to 0.25
- narrowing_matrix_second: bfloat16 [2, 2048, 512], replicated, may hold values from -0.125 to 0.125
- sky_clarity_marks: int32 [8, 4], replicated, may hold values 0 or 1
Outputs:
- features: bfloat16 [512, 256, 512], P('row', 'col')
Inputs may be any that keep to these rules, and one draw needn't show every extreme that they name: `sky_clarity_marks`: 1 marks a tile of 64 x 64 section-two pixels whose blocks are applied, 0 a cloudy tile that passes through section two unchanged.
All inputs are finite; a program needn't handle non-finite values.
Results may differ from a plain program's by a relative error of at most 0.022.
Values may be sent and summed in bfloat16 or wider, within the bound.
No kernel may reach another device: no remote copies, remote signals or barrier semaphores. Data moves between devices by JAX's collectives and lax.ppermute only.
A program may use at most 128 MiB of HBM per device.

v0:
```python
import functools

import jax
import jax.numpy as jnp
import numpy as np
from jax import lax
from jax.experimental import pallas as pl
from jax.experimental.pallas import tpu as pltpu
from jax.sharding import PartitionSpec as P

TILE2 = 64
EPS = 1e-06
F32 = jnp.float32
BF16 = jnp.bfloat16
S = 16
PAD = 8
RING = 6


def spread(width):
    planes = width // S
    hot = np.zeros((planes + 6, S, width), np.float32)
    for t in range(-3, planes + 3):
        for s in range(S):
            c = planes * s + t
            if 0 <= c < width:
                hot[t + 3, s, c] = 1
    return hot.reshape((planes + 6) * S, width)


def pick(width, columns):
    planes = width // S
    hot = np.zeros((len(columns), width), np.float32)
    for j, c in enumerate(columns):
        s, t = divmod(c + PAD, planes)
        hot[j, t * S + s] = 1
    return hot


def dot(a, b):
    return jnp.dot(a, b, preferred_element_type=F32)


def spread_taps(taps_ref, layer, wide_ref):
    taps = taps_ref[layer].astype(F32)
    for tap in range(49):
        row = jnp.broadcast_to(taps[tap : tap + 1], (S, taps.shape[1]))
        wide_ref[tap] = row.astype(BF16)


def depthwise(field_ref, row, wide_ref, planes, lanes):
    total = None
    for a in range(7):
        line = field_ref[row + a, :, :, lanes]
        p = [line[b : b + planes] * wide_ref[7 * a + b, :, lanes][None] for b in range(7)]
        part = ((p[0] + p[1]) + (p[2] + p[3])) + ((p[4] + p[5]) + p[6])
        part = part.astype(F32)
        total = part if total is None else total + part
    return total


def normalize(parts):
    depth = 128 * len(parts)
    mean = jnp.sum(functools.reduce(jnp.add, parts), axis=-1, keepdims=True) / depth
    centred = [p - mean for p in parts]
    squares = functools.reduce(jnp.add, [c * c for c in centred])
    variance = jnp.sum(squares, axis=-1, keepdims=True) / depth
    scale = lax.rsqrt(variance + EPS)
    return jnp.concatenate([c * scale for c in centred], axis=-1).astype(BF16)


def gelu(h):
    return (0.5 * h * (1.0 + lax.erf(h * np.float32(0.5**0.5)))).astype(BF16)


def mlp(flat, w_in_ref, w_out_ref, layer, step):
    hidden = w_in_ref.shape[2]
    total = None
    for c in range(0, hidden, step):
        h = gelu(dot(flat, w_in_ref[layer, :, c : c + step]))
        part = dot(h, w_out_ref[layer, c : c + step, :])
        total = part if total is None else total + part
    return total


def store_planes(field_ref, row, values, planes):
    field_ref[row, 3 : 3 + planes] = values.astype(BF16)
    for j in range(3):
        field_ref[row, j] = pltpu.roll(values[planes - 3 + j], 1, 0).astype(BF16)
        field_ref[row, 3 + planes + j] = pltpu.roll(values[j], S - 1, 0).astype(BF16)


def column_index(planes):
    t = lax.broadcasted_iota(jnp.int32, (planes, S, 1), 0)
    s = lax.broadcasted_iota(jnp.int32, (planes, S, 1), 1)
    return planes * s + t - PAD


def section_one(
    bounds_ref, x_ref, spread_ref, pick_ref, taps_ref, w_in_ref, w_out_ref, stride_ref,
    out_ref, field0, field1, wide, patches,
):
    rows = x_ref.shape[0] - 2 * RING
    width, depth = x_ref.shape[1:]
    planes = width // S
    pixels = planes * S
    halves = [pl.ds(128 * c, 128) for c in range(depth // 128)]
    columns = column_index(planes)
    inside = (columns >= bounds_ref[2]) & (columns < bounds_ref[3])

    def permute(r, carry):
        field0[r] = dot(spread_ref[...], x_ref[r]).astype(BF16).reshape(planes + 6, S, depth)
        return carry

    lax.fori_loop(0, rows + 2 * RING, permute, 0)

    def block(field_ref, layer, row):
        parts = [
            jnp.concatenate([depthwise(field_ref, row + i, wide, planes, h) for i in range(2)], 0)
            for h in halves
        ]
        flat = normalize(parts).reshape(2 * pixels, depth)
        branch = mlp(flat, w_in_ref, w_out_ref, layer, 256).reshape(2, planes, S, depth)
        return [field_ref[row + i + 3, 3 : 3 + planes].astype(F32) + branch[i] for i in range(2)]

    spread_taps(taps_ref, 0, wide)

    def first(g, carry):
        values = block(field0, 0, 2 * g)
        for i in range(2):
            r = 2 * g + i - 3
            keep = inside & (r >= bounds_ref[0]) & (r < bounds_ref[1])
            store_planes(field1, 2 * g + i, jnp.where(keep, values[i], 0.0), planes)
        return carry

    lax.fori_loop(0, (rows + 6) // 2, first, 0)
    spread_taps(taps_ref, 1, wide)

    def second(g, carry):
        values = block(field1, 1, 2 * g)
        for dy in range(2):
            rounded = values[dy].astype(BF16).astype(F32)
            normed = normalize([rounded[:, :, 128 * c : 128 * c + 128] for c in range(depth // 128)])
            chosen = dot(pick_ref[...], normed.reshape(pixels, depth)).astype(BF16)
            half = chosen.shape[0] // 2
            for dx in range(2):
                at = (2 * dy + dx) * depth
                patches[g, :, at : at + depth] = chosen[dx * half : (dx + 1) * half]
        return carry

    lax.fori_loop(0, rows // 2, second, 0)
    coarse = dot(patches[...].reshape(-1, 4 * depth), stride_ref[...])
    out_ref[...] = coarse.astype(BF16).reshape(out_ref.shape)


def section_two(
    bounds_ref, flags_ref, z_ref, spread_ref, pick_ref, taps_ref, w_in_ref, w_out_ref,
    out_ref, field0, field1, wide, flats, total,
):
    rows, cols = out_ref.shape[:2]
    width, depth = z_ref.shape[1:]
    hidden = w_in_ref.shape[2]
    planes = width // S
    pixels = planes * S
    groups = [pl.ds(128 * c, 128) for c in range(depth // 128)]
    step = 512

    @pl.when(flags_ref[4] == 0)
    def _():
        out_ref[...] = z_ref[RING : RING + rows, PAD : PAD + cols, :]

    @pl.when(flags_ref[4] != 0)
    def _():
        columns = column_index(planes)
        inside = (columns >= bounds_ref[2]) & (columns < bounds_ref[3])

        def permute(r, carry):
            field0[r] = dot(spread_ref[...], z_ref[r]).astype(BF16).reshape(planes + 6, S, depth)
            return carry

        lax.fori_loop(0, rows + 2 * RING, permute, 0)

        def block(field_ref, layer, count):
            spread_taps(taps_ref, layer, wide)

            def one(r, carry):
                parts = [depthwise(field_ref, r, wide, planes, c) for c in groups]
                flats[r] = normalize(parts).reshape(pixels, depth)
                return carry

            lax.fori_loop(0, count, one, 0)
            half = count // 2
            for q in range(2):
                flat = flats[q * half : (q + 1) * half].reshape(half * pixels, depth)
                branch = mlp(flat, w_in_ref, w_out_ref, layer, step)
                total[q * half : (q + 1) * half] = branch.reshape(half, planes, S, depth)

        block(field0, 0, rows + 6)

        def merge(band):
            def one(r, carry):
                old = field0[r + 3, 3 : 3 + planes].astype(F32)
                left, mid, right = [flags_ref[3 * band + k] for k in range(3)]
                flag = jnp.where(columns < 0, left, jnp.where(columns < cols, mid, right))
                new = jnp.where(flag != 0, old + total[r], old)
                own = r - 3
                keep = inside & (own >= bounds_ref[0]) & (own < bounds_ref[1])
                store_planes(field1, r, jnp.where(keep, new, 0.0), planes)
                return carry

            return one

        lax.fori_loop(0, 3, merge(0), 0)
        lax.fori_loop(3, rows + 3, merge(1), 0)
        lax.fori_loop(rows + 3, rows + 6, merge(2), 0)
        block(field1, 1, rows)

        def finish(r, carry):
            new = field1[r + 3, 3 : 3 + planes].astype(F32) + total[r]
            new = new.astype(BF16).reshape(pixels, depth)
            out_ref[r] = dot(pick_ref[...], new).astype(BF16)
            return carry

        lax.fori_loop(0, rows, finish, 0)


def with_halo(cells):
    for axis, dim, width in (("col", 1, PAD), ("row", 0, RING)):
        ends = lax.axis_size(axis) - 1
        head = lax.slice_in_dim(cells, 0, width, axis=dim)
        tail = lax.slice_in_dim(cells, cells.shape[dim] - width, cells.shape[dim], axis=dim)
        before = lax.ppermute(tail, axis, [(i, i + 1) for i in range(ends)])
        after = lax.ppermute(head, axis, [(i + 1, i) for i in range(ends)])
        cells = jnp.concatenate([before, cells, after], axis=dim)
    return cells


def call(kernel, name, out_shape, scalars, arrays, scratch):
    return pl.pallas_call(
        kernel,
        name=name,
        out_shape=out_shape,
        in_specs=[pl.BlockSpec(memory_space=pltpu.SMEM) for _ in scalars]
        + [pl.BlockSpec(memory_space=pltpu.VMEM) for _ in arrays],
        out_specs=pl.BlockSpec(memory_space=pltpu.VMEM),
        scratch_shapes=[pltpu.VMEM(shape, dtype) for shape, dtype in scratch],
        compiler_params=pltpu.CompilerParams(vmem_limit_bytes=56 * 1024 * 1024),
    )(*scalars, *arrays)


def run_one(bounds, padded, taps, w_in, w_out, stride):
    rows, width, depth = padded.shape
    rows -= 2 * RING
    planes = width // S
    half = (width - 2 * PAD) // 2
    wide_depth = stride.shape[1]
    columns = [2 * j + dx for dx in range(2) for j in range(half)]
    return call(
        section_one,
        "section_one",
        jax.ShapeDtypeStruct((rows // 2, half, wide_depth), BF16),
        [bounds],
        [padded, jnp.asarray(spread(width), BF16), jnp.asarray(pick(width, columns), BF16),
         taps, w_in, w_out, stride],
        [
            ((rows + 2 * RING, planes + 6, S, depth), BF16),
            ((rows + 6, planes + 6, S, depth), BF16),
            ((49, S, depth), BF16),
            ((rows // 2, half, 4 * depth), BF16),
        ],
    )


def run_two(bounds, flags, padded, taps, w_in, w_out):
    rows, width, depth = padded.shape
    rows -= 2 * RING
    cols = width - 2 * PAD
    planes = width // S
    return call(
        section_two,
        "section_two",
        jax.ShapeDtypeStruct((rows, cols, depth), BF16),
        [bounds, flags],
        [padded, jnp.asarray(spread(width), BF16), jnp.asarray(pick(width, range(cols)), BF16),
         taps, w_in, w_out],
        [
            ((rows + 2 * RING, planes + 6, S, depth), BF16),
            ((rows + 6, planes + 6, S, depth), BF16),
            ((49, S, depth), BF16),
            ((rows + 6, planes * S, depth), BF16),
            ((rows + 6, planes, S, depth), F32),
        ],
    )


def edges(rows, cols):
    i, j = lax.axis_index("row"), lax.axis_index("col")
    last_i, last_j = lax.axis_size("row") - 1, lax.axis_size("col") - 1
    far = 1 << 20
    return jnp.stack([
        jnp.where(i == 0, 0, -far),
        jnp.where(i == last_i, rows, far),
        jnp.where(j == 0, 0, -far),
        jnp.where(j == last_j, cols, far),
    ]).astype(jnp.int32)


def tile_flags(marks, rows, cols):
    i, j = lax.axis_index("row") * rows, lax.axis_index("col") * cols
    down = jnp.stack([i - 1, i, i + rows]) // TILE2
    across = jnp.stack([j - 1, j, j + cols]) // TILE2
    down = jnp.clip(down, 0, marks.shape[0] - 1)
    across = jnp.clip(across, 0, marks.shape[1] - 1)
    return (marks[down][:, across] == 1).astype(jnp.int32).reshape(9)


def per_device(
    input_picture,
    spatial_taps_first,
    widening_matrix_first,
    narrowing_matrix_first,
    stride_kernel_matrix,
    spatial_taps_second,
    widening_matrix_second,
    narrowing_matrix_second,
    sky_clarity_marks,
):
    rows, cols = input_picture.shape[:2]
    coarse = run_one(
        edges(rows, cols),
        with_halo(input_picture),
        spatial_taps_first,
        widening_matrix_first,
        narrowing_matrix_first,
        stride_kernel_matrix,
    )
    return run_two(
        edges(rows // 2, cols // 2),
        tile_flags(sky_clarity_marks, rows // 2, cols // 2),
        with_halo(coarse),
        spatial_taps_second,
        widening_matrix_second,
        narrowing_matrix_second,
    )


def solution(mesh):
    placed = (P("row", "col", None), P(), P(), P(), P(), P(), P(), P(), P())
    return jax.shard_map(
        per_device, mesh=mesh, in_specs=placed, out_specs=P("row", "col", None), check_vma=False
    )
```

profile of v0, /device:TPU:26, one launch (start us, length us, event | category | flops | bytes accessed | tf_op | source)
XLA Modules:
  0.0 172.5 jit_solution(9889077151391630850)
XLA Ops:
  0.0 0.9 fusion.3
  0.9 1.3 collective-permute-start
  2.2 4.5 %collective-permute-start.1 = (bf16[16,8,256]{2,1,0:T(8,128)(2,1)S(1)}, bf16[16,8,256]{2,1,0:T(8,128)(2,1)S(1)}, u32[]{:S(2)}, u32[]{:S(2)}) collective-permute-start(bf16[16,8,256]{2,1,0:T(8,128)(2,1)S(1)} %get-tuple-element.7), channel_id=1, source_target_pairs={{1,0},{2,1},{3,2},{5,4},{6,5},{7,6},{9,8},{10,9},{11,10},{13,12},{... | collective-permute-start | bytes 196616 | tf_op jit(solution)/shard_map/ppermute | solution.py:233
  6.7 0.3 collective-permute-done
  7.1 1.3 constant_dynamic-update-slice_fusion.1
  8.4 0.3 collective-permute-done.1
  8.7 6.1 %collective-permute-start.3 = (bf16[6,144,256]{2,1,0:T(8,128)(2,1)S(1)}, bf16[6,144,256]{2,1,0:T(8,128)(2,1)S(1)}, u32[]{:S(2)}, u32[]{:S(2)}) collective-permute-start(bf16[6,144,256]{2,1,0:T(8,128)(2,1)S(1)} %get-tuple-element.6), channel_id=1, source_target_pairs={{4,0},{8,4},{12,8},{16,12},{20,16},{24,20},{28,24},{32,28},{36,32}... | collective-permute-start | bytes 1327112 | tf_op jit(solution)/shard_map/ppermute | solution.py:233
  14.8 1.9 %collective-permute-start.2 = (bf16[6,144,256]{2,1,0:T(8,128)(2,1)S(1)}, bf16[6,144,256]{2,1,0:T(8,128)(2,1)S(1)}, u32[]{:S(2)}, u32[]{:S(2)}) collective-permute-start(bf16[6,144,256]{2,1,0:T(8,128)(2,1)S(1)} %get-tuple-element.5), channel_id=1, source_target_pairs={{0,4},{4,8},{8,12},{12,16},{16,20},{20,24},{24,28},{28,32},{32,36}... | collective-permute-start | bytes 1327112 | tf_op jit(solution)/shard_map/ppermute | solution.py:232
  16.8 0.6 copy.17.taps_ref
  17.4 0.6 pad_add_fusion.3.bounds_ref
  18.0 2.6 %collective-permute-done.3 = bf16[6,144,256]{2,1,0:T(8,128)(2,1)S(1)} collective-permute-done((bf16[6,144,256]{2,1,0:T(8,128)(2,1)S(1)}, bf16[6,144,256]{2,1,0:T(8,128)(2,1)S(1)}, u32[]{:S(2)}, u32[]{:S(2)}) %collective-permute-start.3) | collective-permute-done | bytes 442400 | tf_op jit(solution)/shard_map/ppermute | solution.py:233
  20.6 5.9 %collective-permute-done.2 = bf16[6,144,256]{2,1,0:T(8,128)(2,1)S(1)} collective-permute-done((bf16[6,144,256]{2,1,0:T(8,128)(2,1)S(1)}, bf16[6,144,256]{2,1,0:T(8,128)(2,1)S(1)}, u32[]{:S(2)}, u32[]{:S(2)}) %collective-permute-start.2) | collective-permute-done | bytes 442400 | tf_op jit(solution)/shard_map/ppermute | solution.py:232
  26.5 1.6 pad_maximum_fusion.x_ref
  28.1 57.7 %section_one.1 = bf16[8,64,512]{2,1,0:T(8,128)(2,1)} custom-call(s32[4]{0:T(128)} %pad_add_fusion.3.bounds_ref, bf16[28,144,256]{2,1,0:T(8,128)(2,1)} %pad_maximum_fusion.x_ref, bf16[240,144]{1,0:T(8,128)(2,1)} %constant.65.clone.spread_ref, bf16[128,144]{1,0:T(8,128)(2,1)} %constant.66.clone.pick_ref, bf16[2,49,256]{2,1,0:T(8,128)(2,1)} %copy.17.taps_ref, ...), custom_call_target="tpu_custom_call" | custom-call | tf_op jit(solution)/shard_map/section_one/pallas_call | solution.py:239
  85.8 0.9 fusion.5
  86.7 3.9 %collective-permute-start.5 = (bf16[8,8,512]{2,1,0:T(8,128)(2,1)S(1)}, bf16[8,8,512]{2,1,0:T(8,128)(2,1)S(1)}, u32[]{:S(2)}, u32[]{:S(2)}) collective-permute-start(bf16[8,8,512]{2,1,0:T(8,128)(2,1)S(1)} %get-tuple-element.12), channel_id=1, source_target_pairs={{1,0},{2,1},{3,2},{5,4},{6,5},{7,6},{9,8},{10,9},{11,10},{13,12},{... | collective-permute-start | bytes 196616 | tf_op jit(solution)/shard_map/ppermute | solution.py:233
  90.6 1.3 collective-permute-start.4
  92.1 0.5 collective-permute-done.5
  92.5 4.3 %collective-permute-done.4 = bf16[8,8,512]{2,1,0:T(8,128)(2,1)S(1)} collective-permute-done((bf16[8,8,512]{2,1,0:T(8,128)(2,1)S(1)}, bf16[8,8,512]{2,1,0:T(8,128)(2,1)S(1)}, u32[]{:S(2)}, u32[]{:S(2)}) %collective-permute-start.4) | collective-permute-done | bytes 65568 | tf_op jit(solution)/shard_map/ppermute | solution.py:232
  96.8 1.1 pad_maximum_fusion.2
  98.0 1.9 %collective-permute-start.7 = (bf16[6,80,512]{2,1,0:T(8,128)(2,1)S(1)}, bf16[6,80,512]{2,1,0:T(8,128)(2,1)S(1)}, u32[]{:S(2)}, u32[]{:S(2)}) collective-permute-start(bf16[6,80,512]{2,1,0:T(8,128)(2,1)S(1)} %get-tuple-element.10), channel_id=1, source_target_pairs={{4,0},{8,4},{12,8},{16,12},{20,16},{24,20},{28,24},{32,28},{36,32}... | collective-permute-start | bytes 1474568 | tf_op jit(solution)/shard_map/ppermute | solution.py:233
  99.9 2.4 %collective-permute-start.6 = (bf16[6,80,512]{2,1,0:T(8,128)(2,1)S(1)}, bf16[6,80,512]{2,1,0:T(8,128)(2,1)S(1)}, u32[]{:S(2)}, u32[]{:S(2)}) collective-permute-start(bf16[6,80,512]{2,1,0:T(8,128)(2,1)S(1)} %get-tuple-element.9), channel_id=1, source_target_pairs={{0,4},{4,8},{8,12},{12,16},{16,20},{20,24},{24,28},{28,32},{32,36}... | collective-permute-start | bytes 1474568 | tf_op jit(solution)/shard_map/ppermute | solution.py:232
  102.5 0.6 gather_fusion
  103.1 0.1 copy.15
  103.2 0.6 gather_fusion.1
  103.8 0.6 reshape.420.flags_ref
  104.4 0.7 copy.18.taps_ref
  105.1 0.6 pad_add_fusion.bounds_ref
  105.7 0.5 collective-permute-done.7
  106.2 5.9 %collective-permute-done.6 = bf16[6,80,512]{2,1,0:T(8,128)(2,1)S(1)} collective-permute-done((bf16[6,80,512]{2,1,0:T(8,128)(2,1)S(1)}, bf16[6,80,512]{2,1,0:T(8,128)(2,1)S(1)}, u32[]{:S(2)}, u32[]{:S(2)}) %collective-permute-start.6) | collective-permute-done | bytes 491552 | tf_op jit(solution)/shard_map/ppermute | solution.py:232
  112.2 1.3 pad_maximum_fusion.1.z_ref
  113.5 59.0 %section_two.1 = bf16[8,64,512]{2,1,0:T(8,128)(2,1)} custom-call(s32[4]{0:T(128)} %pad_add_fusion.bounds_ref, s32[9]{0:T(128)} %reshape.420.flags_ref, bf16[20,80,512]{2,1,0:T(8,128)(2,1)} %pad_maximum_fusion.1.z_ref, bf16[176,80]{1,0:T(8,128)(2,1)} %constant.67.clone.spread_ref, bf16[64,80]{1,0:T(8,128)(2,1)} %constant.68.clone.pick_ref, ...), custom_call_target="tpu_custom_call" | custom-call | tf_op jit(solution)/shard_map/section_two/pallas_call | solution.py:239
  (18 shorter events, 0.5 us)
Async XLA Ops:
  0.9 6.2 %collective-permute-start = (bf16[16,8,256]{2,1,0:T(8,128)(2,1)S(1)}, bf16[16,8,256]{2,1,0:T(8,128)(2,1)S(1)}, u32[]{:S(2)}, u32[]{:S(2)}) collective-permute-start(bf16[16,8,256]{2,1,0:T(8,128)(2,1)S(1)} %get-tuple-element.8), channel_id=1, source_target_pairs={{0,1},{1,2},{2,3},{4,5},{5,6},{6,7},{8,9},{9,10},{10,11},{12,13},{... | collective-permute-start | bytes 196616 | tf_op jit(solution)/shard_map/ppermute | solution.py:232
  2.2 6.4 %collective-permute-start.1 = (bf16[16,8,256]{2,1,0:T(8,128)(2,1)S(1)}, bf16[16,8,256]{2,1,0:T(8,128)(2,1)S(1)}, u32[]{:S(2)}, u32[]{:S(2)}) collective-permute-start(bf16[16,8,256]{2,1,0:T(8,128)(2,1)S(1)} %get-tuple-element.7), channel_id=1, source_target_pairs={{1,0},{2,1},{3,2},{5,4},{6,5},{7,6},{9,8},{10,9},{11,10},{13,12},{... | collective-permute-start | bytes 196616 | tf_op jit(solution)/shard_map/ppermute | solution.py:233
  7.1 9.7 %copy-start.2 = (bf16[2,49,256]{2,0,1:T(2,128)(2,1)S(1)}, bf16[2,49,256]{2,0,1:T(2,128)(2,1)}, u32[]{:S(2)}) copy-start(bf16[2,49,256]{2,0,1:T(2,128)(2,1)} %param.14) | copy-start | bytes 150532
  8.7 11.9 %collective-permute-start.3 = (bf16[6,144,256]{2,1,0:T(8,128)(2,1)S(1)}, bf16[6,144,256]{2,1,0:T(8,128)(2,1)S(1)}, u32[]{:S(2)}, u32[]{:S(2)}) collective-permute-start(bf16[6,144,256]{2,1,0:T(8,128)(2,1)S(1)} %get-tuple-element.6), channel_id=1, source_target_pairs={{4,0},{8,4},{12,8},{16,12},{20,16},{24,20},{28,24},{32,28},{36,32}... | collective-permute-start | bytes 1327112 | tf_op jit(solution)/shard_map/ppermute | solution.py:233
  14.8 11.7 %collective-permute-start.2 = (bf16[6,144,256]{2,1,0:T(8,128)(2,1)S(1)}, bf16[6,144,256]{2,1,0:T(8,128)(2,1)S(1)}, u32[]{:S(2)}, u32[]{:S(2)}) collective-permute-start(bf16[6,144,256]{2,1,0:T(8,128)(2,1)S(1)} %get-tuple-element.5), channel_id=1, source_target_pairs={{0,4},{4,8},{8,12},{12,16},{16,20},{20,24},{24,28},{28,32},{32,36}... | collective-permute-start | bytes 1327112 | tf_op jit(solution)/shard_map/ppermute | solution.py:232
  86.7 5.8 %collective-permute-start.5 = (bf16[8,8,512]{2,1,0:T(8,128)(2,1)S(1)}, bf16[8,8,512]{2,1,0:T(8,128)(2,1)S(1)}, u32[]{:S(2)}, u32[]{:S(2)}) collective-permute-start(bf16[8,8,512]{2,1,0:T(8,128)(2,1)S(1)} %get-tuple-element.12), channel_id=1, source_target_pairs={{1,0},{2,1},{3,2},{5,4},{6,5},{7,6},{9,8},{10,9},{11,10},{13,12},{... | collective-permute-start | bytes 196616 | tf_op jit(solution)/shard_map/ppermute | solution.py:233
  90.6 6.2 %collective-permute-start.4 = (bf16[8,8,512]{2,1,0:T(8,128)(2,1)S(1)}, bf16[8,8,512]{2,1,0:T(8,128)(2,1)S(1)}, u32[]{:S(2)}, u32[]{:S(2)}) collective-permute-start(bf16[8,8,512]{2,1,0:T(8,128)(2,1)S(1)} %get-tuple-element.11), channel_id=1, source_target_pairs={{0,1},{1,2},{2,3},{4,5},{5,6},{6,7},{8,9},{9,10},{10,11},{12,13},{... | collective-permute-start | bytes 196616 | tf_op jit(solution)/shard_map/ppermute | solution.py:232
  92.0 10.4 %copy-start.3 = (s32[8,4]{0,1:T(4,128)S(1)}, s32[8,4]{0,1:T(4,128)}, u32[]{:S(2)}) copy-start(s32[8,4]{0,1:T(4,128)} %param.21) | copy-start | bytes 388
  92.0 12.4 %copy-start.1 = (bf16[2,49,512]{2,0,1:T(2,128)(2,1)S(1)}, bf16[2,49,512]{2,0,1:T(2,128)(2,1)}, u32[]{:S(2)}) copy-start(bf16[2,49,512]{2,0,1:T(2,128)(2,1)} %param.18) | copy-start | bytes 301060
  92.0 20.1 %copy-start = (bf16[8,64,512]{2,1,0:T(8,128)(2,1)S(1)}, bf16[8,64,512]{2,1,0:T(8,128)(2,1)}, u32[]{:S(2)}) copy-start(bf16[8,64,512]{2,1,0:T(8,128)(2,1)} %section_one.1) | copy-start | bytes 1572868
  98.0 8.3 %collective-permute-start.7 = (bf16[6,80,512]{2,1,0:T(8,128)(2,1)S(1)}, bf16[6,80,512]{2,1,0:T(8,128)(2,1)S(1)}, u32[]{:S(2)}, u32[]{:S(2)}) collective-permute-start(bf16[6,80,512]{2,1,0:T(8,128)(2,1)S(1)} %get-tuple-element.10), channel_id=1, source_target_pairs={{4,0},{8,4},{12,8},{16,12},{20,16},{24,20},{28,24},{32,28},{36,32}... | collective-permute-start | bytes 1474568 | tf_op jit(solution)/shard_map/ppermute | solution.py:233
  99.9 12.3 %collective-permute-start.6 = (bf16[6,80,512]{2,1,0:T(8,128)(2,1)S(1)}, bf16[6,80,512]{2,1,0:T(8,128)(2,1)S(1)}, u32[]{:S(2)}, u32[]{:S(2)}) collective-permute-start(bf16[6,80,512]{2,1,0:T(8,128)(2,1)S(1)} %get-tuple-element.9), channel_id=1, source_target_pairs={{0,4},{4,8},{8,12},{12,16},{16,20},{20,24},{24,28},{28,32},{32,36}... | collective-permute-start | bytes 1474568 | tf_op jit(solution)/shard_map/ppermute | solution.py:232
where the time goes:
time: 173 us
  Pallas kernels  117 us (68%)
  starting transfers between devices  23.4 us (14%)
  waiting for transfers between devices  20.3 us (12%)
  local copies, waits for them, and re-layouts  6.5 us (4%)
  other arithmetic  5.45 us (3%)
    pallas_call x2, Pallas kernels, call(): pl.pallas_call(kernel, name=name, out_shape=out_shape, in_specs=[pl.Block...  117 us
    ppermute x4, starting transfers between devices, with_halo(): after = lax.ppermute(head, axis, [(i + 1, i) for i in range(ends)])  16.5 us
    ppermute x4, waiting for transfers between devices, with_halo(): before = lax.ppermute(tail, axis, [(i, i + 1) for i in range(ends)])  16.4 us
    ppermute x4, starting transfers between devices, with_halo(): before = lax.ppermute(tail, axis, [(i, i + 1) for i in range(ends)])  6.91 us
    concatenate x3, other arithmetic, with_halo(): cells = jnp.concatenate([before, cells, after], axis=dim)  4 us
    ppermute x4, waiting for transfers between devices, with_halo(): after = lax.ppermute(head, axis, [(i + 1, i) for i in range(ends)])  3.82 us
  transfers between devices with their start and end apart: 8, of which 8 were waited for; matrix products, arithmetic and copies ran while one was open for 3% of the time, Pallas kernels for 0%

commit v1 on v0

v1 whole, which is shorter than its diff:
```python
import functools

import jax
import jax.numpy as jnp
import numpy as np
from jax import lax
from jax.experimental import pallas as pl
from jax.experimental.pallas import tpu as pltpu
from jax.sharding import PartitionSpec as P

TILE2 = 64
EPS = 1e-06
F32 = jnp.float32
BF16 = jnp.bfloat16
S = 16
PAD = 8
RING = 6
GROUP = 2


def spread(width):
    planes = width // S
    hot = np.zeros((planes + 6, S, width), np.float32)
    for t in range(-3, planes + 3):
        for s in range(S):
            c = planes * s + t
            if 0 <= c < width:
                hot[t + 3, s, c] = 1
    return hot.reshape((planes + 6) * S, width)


def pick(width, columns):
    planes = width // S
    hot = np.zeros((len(columns), width), np.float32)
    for j, c in enumerate(columns):
        s, t = divmod(c + PAD, planes)
        hot[j, t * S + s] = 1
    return hot


def dot(a, b):
    return jnp.dot(a, b, preferred_element_type=F32)


def spread_taps(taps_ref, layer, wide_ref):
    taps = taps_ref[layer].astype(F32)
    for tap in range(49):
        wide_ref[tap] = jnp.broadcast_to(taps[tap : tap + 1], wide_ref.shape[1:])


def depthwise(field_ref, row, wide_ref, planes, lanes):
    total = [None] * planes
    for a in range(7):
        line = field_ref[row + a, :, :, lanes].astype(F32).reshape(planes + 6, S // 8, 8, 128)
        for b in range(7):
            tap = wide_ref[7 * a + b, :, lanes][None]
            for t in range(planes):
                p = line[t + b] * tap
                total[t] = p if total[t] is None else total[t] + p
    return jnp.stack(total).reshape(planes, S, 128)


def normalize(parts):
    depth = 128 * len(parts)
    mean = jnp.sum(functools.reduce(jnp.add, parts), axis=-1, keepdims=True) / depth
    centred = [p - mean for p in parts]
    squares = functools.reduce(jnp.add, [c * c for c in centred])
    variance = jnp.sum(squares, axis=-1, keepdims=True) / depth
    scale = lax.rsqrt(variance + EPS)
    return jnp.concatenate([c * scale for c in centred], axis=-1).astype(BF16)


def twice_gelu(h):
    return (h * (1.0 + lax.erf(h * np.float32(0.5**0.5)))).astype(BF16)


def mlp(flat, w_in_ref, w_out_ref, layer, step):
    hidden = w_in_ref.shape[2]
    total = None
    for c in range(0, hidden, step):
        h = twice_gelu(dot(flat, w_in_ref[layer, :, c : c + step]))
        part = dot(h, w_out_ref[layer, c : c + step, :])
        total = part if total is None else total + part
    return 0.5 * total


def run_block(
    field_ref, count, group, layer, taps_ref, w_in_ref, w_out_ref, wide, mixed, step, ahead, emit
):
    planes, depth = field_ref.shape[1] - 6, field_ref.shape[3]
    chunks = depth // 128
    spread_taps(taps_ref, layer, wide)

    def mix(g):
        for i in range(group):
            for c in range(chunks):
                sums = depthwise(field_ref, group * g + i, wide, planes, pl.ds(128 * c, 128))
                mixed[g % 2, c, i] = sums

    def project(g):
        flat = normalize([mixed[g % 2, c] for c in range(chunks)])
        flat = flat.reshape(group * planes * S, depth)
        branch = mlp(flat, w_in_ref, w_out_ref, layer, step)
        emit(g, branch.reshape(group, planes, S, depth))

    mix(0)

    def body(g, carry):
        if ahead:
            mix(g + 1)
        project(g)
        if not ahead:
            mix(g + 1)
        return carry

    last = count // group - 1
    lax.fori_loop(0, last, body, 0)
    project(last)


def store_planes(field_ref, row, values, planes):
    field_ref[row, 3 : 3 + planes] = values.astype(BF16)
    for j in range(3):
        field_ref[row, j] = pltpu.roll(values[planes - 3 + j], 1, 0).astype(BF16)
        field_ref[row, 3 + planes + j] = pltpu.roll(values[j], S - 1, 0).astype(BF16)


def column_index(planes):
    t = lax.broadcasted_iota(jnp.int32, (planes, S, 1), 0)
    s = lax.broadcasted_iota(jnp.int32, (planes, S, 1), 1)
    return planes * s + t - PAD


def permute_rows(spread_ref, source_ref, field_ref, unroll):
    shape = field_ref.shape[1:]

    def one(r, carry):
        field_ref[r] = dot(spread_ref[...], source_ref[r]).astype(BF16).reshape(shape)
        return carry

    lax.fori_loop(0, source_ref.shape[0], one, 0, unroll=unroll)


def picture_edges(place_ref, ends, columns, rows, cols):
    far = 1 << 20
    top = jnp.where(place_ref[0] == 0, 0, -far)
    bottom = jnp.where(place_ref[0] == ends[0], rows, far)
    left = jnp.where(place_ref[1] == 0, 0, -far)
    right = jnp.where(place_ref[1] == ends[1], cols, far)
    return top, bottom, (columns >= left) & (columns < right)


def section_one(
    ends, place_ref, x_ref, spread_ref, pick_ref, taps_ref, w_in_ref, w_out_ref, stride_ref,
    out_ref, field0, field1, wide, mixed, patches,
):
    rows = x_ref.shape[0] - 2 * RING
    width, depth = x_ref.shape[1:]
    planes = width // S
    pixels = planes * S
    columns = column_index(planes)
    top, bottom, inside = picture_edges(place_ref, ends, columns, rows, width - 2 * PAD)
    permute_rows(spread_ref, x_ref, field0, 4)

    def first(g, branch):
        for i in range(GROUP):
            at = GROUP * g + i
            value = field0[at + 3, 3 : 3 + planes].astype(F32) + branch[i]
            keep = inside & (at - 3 >= top) & (at - 3 < bottom)
            store_planes(field1, at, jnp.where(keep, value, 0.0), planes)

    def second(g, branch):
        for dy in range(2):
            value = field1[2 * g + dy + 3, 3 : 3 + planes].astype(F32) + branch[dy]
            value = value.astype(BF16).astype(F32)
            normed = normalize([value[:, :, 128 * c : 128 * c + 128] for c in range(depth // 128)])
            chosen = dot(pick_ref[...], normed.reshape(pixels, depth)).astype(BF16)
            half = chosen.shape[0] // 2
            for dx in range(2):
                at = (2 * dy + dx) * depth
                patches[g, :, at : at + depth] = chosen[dx * half : (dx + 1) * half]

    weights = (taps_ref, w_in_ref, w_out_ref, wide, mixed, 256, False)
    run_block(field0, rows + 6, GROUP, 0, *weights, first)
    run_block(field1, rows, 2, 1, *weights, second)
    coarse = dot(patches[...].reshape(-1, 4 * depth), stride_ref[...])
    out_ref[...] = coarse.astype(BF16).reshape(out_ref.shape)


def section_two(
    ends, place_ref, marks_ref, z_ref, spread_ref, pick_ref, taps_ref, w_in_ref, w_out_ref,
    out_ref, field0, field1, wide, mixed,
):
    rows, cols = out_ref.shape[:2]
    width, depth = z_ref.shape[1:]
    planes = width // S
    pixels = planes * S

    def tile_flag(i, j):
        i = jnp.clip((place_ref[0] * rows + i) // TILE2, 0, marks_ref.shape[0] - 1)
        j = jnp.clip((place_ref[1] * cols + j) // TILE2, 0, marks_ref.shape[1] - 1)
        return marks_ref[i, j]

    clear = tile_flag(0, 0) == 1

    @pl.when(jnp.logical_not(clear))
    def _():
        out_ref[...] = z_ref[RING : RING + rows, PAD : PAD + cols, :]

    @pl.when(clear)
    def _():
        columns = column_index(planes)
        top, bottom, inside = picture_edges(place_ref, ends, columns, rows, cols)
        permute_rows(spread_ref, z_ref, field0, 4)

        def first(g, branch):
            for i in range(GROUP):
                at = GROUP * g + i
                own = at - 3
                old = field0[at + 3, 3 : 3 + planes].astype(F32)
                left, mid, right = [tile_flag(own, j) for j in (-1, 0, cols)]
                flag = jnp.where(columns < 0, left, jnp.where(columns < cols, mid, right))
                new = jnp.where(flag == 1, old + branch[i], old)
                keep = inside & (own >= top) & (own < bottom)
                store_planes(field1, at, jnp.where(keep, new, 0.0), planes)

        def second(g, branch):
            for i in range(2):
                at = 2 * g + i
                new = field1[at + 3, 3 : 3 + planes].astype(F32) + branch[i]
                new = new.astype(BF16).reshape(pixels, depth)
                out_ref[at] = dot(pick_ref[...], new).astype(BF16)

        weights = (taps_ref, w_in_ref, w_out_ref, wide, mixed, 512, True)
        run_block(field0, rows + 6, GROUP, 0, *weights, first)
        run_block(field1, rows, 2, 1, *weights, second)


def with_halo(cells):
    for axis, dim, width in (("col", 1, PAD), ("row", 0, RING)):
        count = lax.axis_size(axis)
        even = lax.axis_index(axis) % 2 == 0
        head = lax.slice_in_dim(cells, 0, width, axis=dim)
        tail = lax.slice_in_dim(cells, cells.shape[dim] - width, cells.shape[dim], axis=dim)
        inner = [(i, i ^ 1) for i in range(count)]
        outer = [(i, (i - 1 ^ 1) + 1) for i in range(1, count - 1)]
        near = lax.ppermute(jnp.where(even, tail, head), axis, inner)
        far = lax.ppermute(jnp.where(even, head, tail), axis, outer)
        before = jnp.where(even, far, near)
        after = jnp.where(even, near, far)
        cells = jnp.concatenate([before, cells, after], axis=dim)
    return cells


def call(kernel, name, out_shape, scalars, arrays, scratch):
    return pl.pallas_call(
        kernel,
        name=name,
        out_shape=out_shape,
        in_specs=[pl.BlockSpec(memory_space=pltpu.SMEM) for _ in scalars]
        + [pl.BlockSpec(memory_space=pltpu.VMEM) for _ in arrays],
        out_specs=pl.BlockSpec(memory_space=pltpu.VMEM),
        scratch_shapes=[pltpu.VMEM(shape, dtype) for shape, dtype in scratch],
        compiler_params=pltpu.CompilerParams(vmem_limit_bytes=56 * 1024 * 1024),
    )(*scalars, *arrays)


def run_one(ends, place, padded, taps, w_in, w_out, stride):
    rows, width, depth = padded.shape
    rows -= 2 * RING
    planes = width // S
    half = (width - 2 * PAD) // 2
    wide_depth = stride.shape[1]
    columns = [2 * j + dx for dx in range(2) for j in range(half)]
    return call(
        functools.partial(section_one, ends),
        "section_one",
        jax.ShapeDtypeStruct((rows // 2, half, wide_depth), BF16),
        [place],
        [padded, jnp.asarray(spread(width), BF16), jnp.asarray(pick(width, columns), BF16),
         taps, w_in, w_out, stride],
        [
            ((rows + 2 * RING, planes + 6, S, depth), BF16),
            ((rows + 6, planes + 6, S, depth), BF16),
            ((49, 8, depth), F32),
            ((2, depth // 128, GROUP, planes, S, 128), F32),
            ((rows // 2, half, 4 * depth), BF16),
        ],
    )


def run_two(ends, place, marks, padded, taps, w_in, w_out):
    rows, width, depth = padded.shape
    rows -= 2 * RING
    cols = width - 2 * PAD
    planes = width // S
    return call(
        functools.partial(section_two, ends),
        "section_two",
        jax.ShapeDtypeStruct((rows, cols, depth), BF16),
        [place, marks],
        [padded, jnp.asarray(spread(width), BF16), jnp.asarray(pick(width, range(cols)), BF16),
         taps, w_in, w_out],
        [
            ((rows + 2 * RING, planes + 6, S, depth), BF16),
            ((rows + 6, planes + 6, S, depth), BF16),
            ((49, 8, depth), F32),
            ((2, depth // 128, GROUP, planes, S, 128), F32),
        ],
    )


def per_device(
    input_picture,
    spatial_taps_first,
    widening_matrix_first,
    narrowing_matrix_first,
    stride_kernel_matrix,
    spatial_taps_second,
    widening_matrix_second,
    narrowing_matrix_second,
    sky_clarity_marks,
):
    axes = ("row", "col")
    place = jnp.stack([lax.axis_index(axis) for axis in axes]).astype(jnp.int32)
    ends = tuple(lax.axis_size(axis) - 1 for axis in axes)
    coarse = run_one(
        ends,
        place,
        with_halo(input_picture),
        spatial_taps_first,
        widening_matrix_first,
        narrowing_matrix_first,
        stride_kernel_matrix,
    )
    return run_two(
        ends,
        place,
        sky_clarity_marks,
        with_halo(coarse),
        spatial_taps_second,
        widening_matrix_second,
        narrowing_matrix_second,
    )


def solution(mesh):
    placed = (P("row", "col", None), P(), P(), P(), P(), P(), P(), P(), P())
    return jax.shard_map(
        per_device, mesh=mesh, in_specs=placed, out_specs=P("row", "col", None), check_vma=False
    )
```

time: 173 us -> 132 us (0.76)
  the two profiles are of different devices: /device:TPU:26 before, /device:TPU:6 now
where the time goes in v1:
time: 132 us; the launch traced here: 131 us
  Pallas kernels  85.1 us (64%)
  starting transfers between devices  21.2 us (16%)
  waiting for transfers between devices  13.7 us (10%)
  other arithmetic  8 us (6%)
  local copies, waits for them, and re-layouts  2.79 us (2%)
    pallas_call x2, Pallas kernels, call(): pl.pallas_call(kernel, name=name, out_shape=out_shape, in_specs=[pl.Block...  85.1 us
    ppermute x4, starting transfers between devices, with_halo(): far = lax.ppermute(jnp.where(even, head, tail), axis, outer)  12.9 us
    ppermute x4, waiting for transfers between devices, with_halo(): far = lax.ppermute(jnp.where(even, head, tail), axis, outer)  9.19 us
    ppermute x4, starting transfers between devices, with_halo(): near = lax.ppermute(jnp.where(even, tail, head), axis, inner)  8.37 us
    ppermute x4, waiting for transfers between devices, with_halo(): near = lax.ppermute(jnp.where(even, tail, head), axis, inner)  4.49 us
    concatenate x3, other arithmetic, with_halo(): cells = jnp.concatenate([before, cells, after], axis=dim)  3.9 us
    select_n x4, other arithmetic, with_halo(): far = lax.ppermute(jnp.where(even, head, tail), axis, outer)  3.3 us
    unnamed x11, local copies, waits for them, and re-layouts  2.79 us
  transfers between devices with their start and end apart: 8, of which 4 were waited for; matrix products, arithmetic and copies ran while one was open for 3% of the time, Pallas kernels for 0%

profile of v1, /device:TPU:6, one launch (start us, length us, event | category | flops | bytes accessed | tf_op | source)
XLA Modules:
  0.0 130.9 jit_solution(3787789799600565017)
XLA Ops:
  0.0 1.0 broadcast_select_fusion.11
  1.0 0.7 collective-permute-start
  1.7 4.5 %collective-permute-start.1 = (bf16[16,8,256]{2,1,0:T(8,128)(2,1)S(1)}, bf16[16,8,256]{2,1,0:T(8,128)(2,1)S(1)}, u32[]{:S(2)}, u32[]{:S(2)}) collective-permute-start(bf16[16,8,256]{2,1,0:T(8,128)(2,1)S(1)} %get-tuple-element.8), channel_id=1, source_target_pairs={{0,1},{1,0},{2,3},{3,2},{4,5},{5,4},{6,7},{7,6},{8,9},{9,8},{10,11... | collective-permute-start | bytes 196616 | tf_op jit(solution)/shard_map/ppermute | solution.py:247
  6.1 0.0 collective-permute-done
  6.1 2.2 %collective-permute-done.1 = bf16[16,8,256]{2,1,0:T(8,128)(2,1)S(1)} collective-permute-done((bf16[16,8,256]{2,1,0:T(8,128)(2,1)S(1)}, bf16[16,8,256]{2,1,0:T(8,128)(2,1)S(1)}, u32[]{:S(2)}, u32[]{:S(2)}) %collective-permute-start.1) | collective-permute-done | bytes 65568 | tf_op jit(solution)/shard_map/ppermute | solution.py:247
  8.4 1.3 broadcast_select_fusion.7
  9.7 6.3 %collective-permute-start.2 = (bf16[6,144,256]{2,1,0:T(8,128)(2,1)S(1)}, bf16[6,144,256]{2,1,0:T(8,128)(2,1)S(1)}, u32[]{:S(2)}, u32[]{:S(2)}) collective-permute-start(bf16[6,144,256]{2,1,0:T(8,128)(2,1)S(1)} %get-tuple-element.5), channel_id=1, source_target_pairs={{4,8},{8,4},{12,16},{16,12},{20,24},{24,20},{28,32},{32,28},{36,40... | collective-permute-start | bytes 1327112 | tf_op jit(solution)/shard_map/ppermute | solution.py:248
  16.0 0.1 collective-permute-start.3
  16.1 1.4 %copy.14.taps_ref = bf16[2,49,256]{2,1,0:T(8,128)(2,1)} copy(bf16[2,49,256]{2,0,1:T(2,128)(2,1)} %param.14) | data formatting | bytes 100352 | tf_op args[1]
  17.6 0.6 pad_add_fusion.place_ref
  18.2 3.8 %collective-permute-done.2 = bf16[6,144,256]{2,1,0:T(8,128)(2,1)S(1)} collective-permute-done((bf16[6,144,256]{2,1,0:T(8,128)(2,1)S(1)}, bf16[6,144,256]{2,1,0:T(8,128)(2,1)S(1)}, u32[]{:S(2)}, u32[]{:S(2)}) %collective-permute-start.2) | collective-permute-done | bytes 442400 | tf_op jit(solution)/shard_map/ppermute | solution.py:248
  22.0 0.0 collective-permute-done.3
  22.0 0.1 broadcast_select_fusion.5
  22.1 1.5 %pad_maximum_fusion.x_ref = bf16[28,144,256]{2,1,0:T(8,128)(2,1)} fusion(bf16[6,144,256]{2,1,0:T(8,128)(2,1)S(1)} %get-tuple-element.12, bf16[16,8,256]{2,1,0:T(8,128)(2,1)S(1)} %get-tuple-element.20, bf16[16,128,256]{2,1,0:T(8,128)(2,1)S(1)} %copy-done.1, bf16[16,8,256]{2,1,0:T(8,128)(2,1)S(1)} %get-tuple-element.19, bf16[6,144,256]{2,1,0:T(8,128)(2,1)S(1)} %get-tuple-element.11), kind=kLoop, calls=%fused_computation | loop fusion | flops 10321920 | bytes 4128768 | tf_op jit(solution)/shard_map/concatenate | solution.py:251
  23.6 45.4 %section_one.1 = bf16[8,64,512]{2,1,0:T(8,128)(2,1)} custom-call(s32[2]{0:T(128)} %pad_add_fusion.place_ref, bf16[28,144,256]{2,1,0:T(8,128)(2,1)} %pad_maximum_fusion.x_ref, bf16[240,144]{1,0:T(8,128)(2,1)} %constant.39.clone.spread_ref, bf16[128,144]{1,0:T(8,128)(2,1)} %constant.40.clone.pick_ref, bf16[2,49,256]{2,1,0:T(8,128)(2,1)} %copy.14.taps_ref, ...), custom_call_target="tpu_custom_call" | custom-call | tf_op jit(solution)/shard_map/section_one/pallas_call | solution.py:256
  68.9 1.0 broadcast_select_fusion.15
  69.9 0.7 collective-permute-start.4
  70.6 3.5 %collective-permute-start.5 = (bf16[8,8,512]{2,1,0:T(8,128)(2,1)S(1)}, bf16[8,8,512]{2,1,0:T(8,128)(2,1)S(1)}, u32[]{:S(2)}, u32[]{:S(2)}) collective-permute-start(bf16[8,8,512]{2,1,0:T(8,128)(2,1)S(1)} %get-tuple-element.16), channel_id=1, source_target_pairs={{0,1},{1,0},{2,3},{3,2},{4,5},{5,4},{6,7},{7,6},{8,9},{9,8},{10,11... | collective-permute-start | bytes 196616 | tf_op jit(solution)/shard_map/ppermute | solution.py:247
  74.1 0.0 collective-permute-done.4
  74.1 2.2 %collective-permute-done.5 = bf16[8,8,512]{2,1,0:T(8,128)(2,1)S(1)} collective-permute-done((bf16[8,8,512]{2,1,0:T(8,128)(2,1)S(1)}, bf16[8,8,512]{2,1,0:T(8,128)(2,1)S(1)}, u32[]{:S(2)}, u32[]{:S(2)}) %collective-permute-start.5) | collective-permute-done | bytes 65568 | tf_op jit(solution)/shard_map/ppermute | solution.py:247
  76.3 1.1 pad_maximum_fusion.2
  77.4 0.1 broadcast_select_fusion.3
  77.5 5.2 %collective-permute-start.6 = (bf16[6,80,512]{2,1,0:T(8,128)(2,1)S(1)}, bf16[6,80,512]{2,1,0:T(8,128)(2,1)S(1)}, u32[]{:S(2)}, u32[]{:S(2)}) collective-permute-start(bf16[6,80,512]{2,1,0:T(8,128)(2,1)S(1)} %get-tuple-element.13), channel_id=1, source_target_pairs={{4,8},{8,4},{12,16},{16,12},{20,24},{24,20},{28,32},{32,28},{36,40... | collective-permute-start | bytes 1474568 | tf_op jit(solution)/shard_map/ppermute | solution.py:248
  82.8 0.3 collective-permute-start.7
  83.0 0.7 copy.16.taps_ref
  83.7 0.0 copy-done.3
  83.7 0.7 copy.15.marks_ref
  84.4 5.4 %collective-permute-done.6 = bf16[6,80,512]{2,1,0:T(8,128)(2,1)S(1)} collective-permute-done((bf16[6,80,512]{2,1,0:T(8,128)(2,1)S(1)}, bf16[6,80,512]{2,1,0:T(8,128)(2,1)S(1)}, u32[]{:S(2)}, u32[]{:S(2)}) %collective-permute-start.6) | collective-permute-done | bytes 491552 | tf_op jit(solution)/shard_map/ppermute | solution.py:248
  89.8 0.0 collective-permute-done.7
  89.8 0.1 broadcast_select_fusion.1
  89.9 1.3 %pad_maximum_fusion.1.z_ref = bf16[20,80,512]{2,1,0:T(8,128)(2,1)} fusion(bf16[6,80,512]{2,1,0:T(8,128)(2,1)S(1)} %get-tuple-element.10, bf16[8,8,512]{2,1,0:T(8,128)(2,1)S(1)} %get-tuple-element.18, bf16[8,64,512]{2,1,0:T(8,128)(2,1)S(1)} %copy-done, bf16[8,8,512]{2,1,0:T(8,128)(2,1)S(1)} %get-tuple-element.17, bf16[6,80,512]{2,1,0:T(8,128)(2,1)S(1)} %get-tuple-element.9), kind=kLoop, calls=%fused_computation.1 | loop fusion | flops 8192000 | bytes 3276800 | tf_op jit(solution)/shard_map/concatenate | solution.py:251
  91.2 39.7 %section_two.1 = bf16[8,64,512]{2,1,0:T(8,128)(2,1)} custom-call(s32[2]{0:T(128)} %pad_add_fusion.place_ref, s32[8,4]{1,0:T(8,128)} %copy.15.marks_ref, bf16[20,80,512]{2,1,0:T(8,128)(2,1)} %pad_maximum_fusion.1.z_ref, bf16[176,80]{1,0:T(8,128)(2,1)} %constant.41.clone.spread_ref, bf16[64,80]{1,0:T(8,128)(2,1)} %constant.42.clone.pick_ref, ...), custom_call_target="tpu_custom_call" | custom-call | tf_op jit(solution)/shard_map/section_two/pallas_call | solution.py:256
  (9 shorter events, 0.0 us)
Async XLA Ops:
  0.0 22.1 %copy-start.1 = (bf16[16,128,256]{2,1,0:T(8,128)(2,1)S(1)}, bf16[16,128,256]{2,1,0:T(8,128)(2,1)}, u32[]{:S(2)}) copy-start(bf16[16,128,256]{2,1,0:T(8,128)(2,1)} %param.13) | copy-start | bytes 3145732
  1.0 5.2 %collective-permute-start = (bf16[16,8,256]{2,1,0:T(8,128)(2,1)S(1)}, bf16[16,8,256]{2,1,0:T(8,128)(2,1)S(1)}, u32[]{:S(2)}, u32[]{:S(2)}) collective-permute-start(bf16[16,8,256]{2,1,0:T(8,128)(2,1)S(1)} %get-tuple-element.7), channel_id=1, source_target_pairs={{1,2},{2,1},{5,6},{6,5},{9,10},{10,9},{13,14},{14,13},{17,18},{18,... | collective-permute-start | bytes 196616 | tf_op jit(solution)/shard_map/ppermute | solution.py:248
  1.7 6.7 %collective-permute-start.1 = (bf16[16,8,256]{2,1,0:T(8,128)(2,1)S(1)}, bf16[16,8,256]{2,1,0:T(8,128)(2,1)S(1)}, u32[]{:S(2)}, u32[]{:S(2)}) collective-permute-start(bf16[16,8,256]{2,1,0:T(8,128)(2,1)S(1)} %get-tuple-element.8), channel_id=1, source_target_pairs={{0,1},{1,0},{2,3},{3,2},{4,5},{5,4},{6,7},{7,6},{8,9},{9,8},{10,11... | collective-permute-start | bytes 196616 | tf_op jit(solution)/shard_map/ppermute | solution.py:247
  9.7 12.3 %collective-permute-start.2 = (bf16[6,144,256]{2,1,0:T(8,128)(2,1)S(1)}, bf16[6,144,256]{2,1,0:T(8,128)(2,1)S(1)}, u32[]{:S(2)}, u32[]{:S(2)}) collective-permute-start(bf16[6,144,256]{2,1,0:T(8,128)(2,1)S(1)} %get-tuple-element.5), channel_id=1, source_target_pairs={{4,8},{8,4},{12,16},{16,12},{20,24},{24,20},{28,32},{32,28},{36,40... | collective-permute-start | bytes 1327112 | tf_op jit(solution)/shard_map/ppermute | solution.py:248
  16.0 6.0 %collective-permute-start.3 = (bf16[6,144,256]{2,1,0:T(8,128)(2,1)S(1)}, bf16[6,144,256]{2,1,0:T(8,128)(2,1)S(1)}, u32[]{:S(2)}, u32[]{:S(2)}) collective-permute-start(bf16[6,144,256]{2,1,0:T(8,128)(2,1)S(1)} %get-tuple-element.6), channel_id=1, source_target_pairs={{0,4},{4,0},{8,12},{12,8},{16,20},{20,16},{24,28},{28,24},{32,36},... | collective-permute-start | bytes 1327112 | tf_op jit(solution)/shard_map/ppermute | solution.py:247
  68.9 14.1 %copy-start.2 = (bf16[2,49,512]{2,0,1:T(2,128)(2,1)S(1)}, bf16[2,49,512]{2,0,1:T(2,128)(2,1)}, u32[]{:S(2)}) copy-start(bf16[2,49,512]{2,0,1:T(2,128)(2,1)} %param.18) | copy-start | bytes 301060
  68.9 14.8 %copy-start.3 = (s32[8,4]{0,1:T(4,128)S(1)}, s32[8,4]{0,1:T(4,128)}, u32[]{:S(2)}) copy-start(s32[8,4]{0,1:T(4,128)} %param.21) | copy-start | bytes 388
  68.9 20.9 %copy-start = (bf16[8,64,512]{2,1,0:T(8,128)(2,1)S(1)}, bf16[8,64,512]{2,1,0:T(8,128)(2,1)}, u32[]{:S(2)}) copy-start(bf16[8,64,512]{2,1,0:T(8,128)(2,1)} %section_one.1) | copy-start | bytes 1572868
  69.9 4.2 %collective-permute-start.4 = (bf16[8,8,512]{2,1,0:T(8,128)(2,1)S(1)}, bf16[8,8,512]{2,1,0:T(8,128)(2,1)S(1)}, u32[]{:S(2)}, u32[]{:S(2)}) collective-permute-start(bf16[8,8,512]{2,1,0:T(8,128)(2,1)S(1)} %get-tuple-element.15), channel_id=1, source_target_pairs={{1,2},{2,1},{5,6},{6,5},{9,10},{10,9},{13,14},{14,13},{17,18},{18,... | collective-permute-start | bytes 196616 | tf_op jit(solution)/shard_map/ppermute | solution.py:248
  70.6 5.8 %collective-permute-start.5 = (bf16[8,8,512]{2,1,0:T(8,128)(2,1)S(1)}, bf16[8,8,512]{2,1,0:T(8,128)(2,1)S(1)}, u32[]{:S(2)}, u32[]{:S(2)}) collective-permute-start(bf16[8,8,512]{2,1,0:T(8,128)(2,1)S(1)} %get-tuple-element.16), channel_id=1, source_target_pairs={{0,1},{1,0},{2,3},{3,2},{4,5},{5,4},{6,7},{7,6},{8,9},{9,8},{10,11... | collective-permute-start | bytes 196616 | tf_op jit(solution)/shard_map/ppermute | solution.py:247
  77.5 12.3 %collective-permute-start.6 = (bf16[6,80,512]{2,1,0:T(8,128)(2,1)S(1)}, bf16[6,80,512]{2,1,0:T(8,128)(2,1)S(1)}, u32[]{:S(2)}, u32[]{:S(2)}) collective-permute-start(bf16[6,80,512]{2,1,0:T(8,128)(2,1)S(1)} %get-tuple-element.13), channel_id=1, source_target_pairs={{4,8},{8,4},{12,16},{16,12},{20,24},{24,20},{28,32},{32,28},{36,40... | collective-permute-start | bytes 1474568 | tf_op jit(solution)/shard_map/ppermute | solution.py:248
  82.8 7.0 %collective-permute-start.7 = (bf16[6,80,512]{2,1,0:T(8,128)(2,1)S(1)}, bf16[6,80,512]{2,1,0:T(8,128)(2,1)S(1)}, u32[]{:S(2)}, u32[]{:S(2)}) collective-permute-start(bf16[6,80,512]{2,1,0:T(8,128)(2,1)S(1)} %get-tuple-element.14), channel_id=1, source_target_pairs={{0,4},{4,0},{8,12},{12,8},{16,20},{20,16},{24,28},{28,24},{32,36},... | collective-permute-start | bytes 1474568 | tf_op jit(solution)/shard_map/ppermute | solution.py:247

commit v2 on v1

--- a/solution.py
+++ b/solution.py
@@ -237,19 +237,46 @@
 
 
 def with_halo(cells):
-    for axis, dim, width in (("col", 1, PAD), ("row", 0, RING)):
-        count = lax.axis_size(axis)
-        even = lax.axis_index(axis) % 2 == 0
-        head = lax.slice_in_dim(cells, 0, width, axis=dim)
-        tail = lax.slice_in_dim(cells, cells.shape[dim] - width, cells.shape[dim], axis=dim)
-        inner = [(i, i ^ 1) for i in range(count)]
-        outer = [(i, (i - 1 ^ 1) + 1) for i in range(1, count - 1)]
-        near = lax.ppermute(jnp.where(even, tail, head), axis, inner)
-        far = lax.ppermute(jnp.where(even, head, tail), axis, outer)
-        before = jnp.where(even, far, near)
-        after = jnp.where(even, near, far)
-        cells = jnp.concatenate([before, cells, after], axis=dim)
-    return cells
+    axes = ("row", "col")
+    counts = [lax.axis_size(axis) for axis in axes]
+    even = [lax.axis_index(axis) % 2 == 0 for axis in axes]
+
+    def partner(i, count, outer):
+        j = (i - 1 ^ 1) + 1 if outer else i ^ 1
+        return j if 0 <= j < count else None
+
+    def edge(array, dim, outer):
+        width = (RING, PAD)[dim]
+        head = lax.slice_in_dim(array, 0, width, axis=dim)
+        tail = lax.slice_in_dim(array, array.shape[dim] - width, array.shape[dim], axis=dim)
+        return jnp.where(even[dim], *((head, tail) if outer else (tail, head)))
+
+    def swap(array, moves):
+        pairs = []
+        for i in range(counts[0]):
+            for j in range(counts[1]):
+                to = [
+                    at if move is None else partner(at, count, move)
+                    for at, count, move in zip((i, j), counts, moves)
+                ]
+                if None not in to:
+                    pairs.append((i * counts[1] + j, to[0] * counts[1] + to[1]))
+        return lax.ppermute(array, axes, pairs)
+
+    def sides(dim, inner, outer):
+        return jnp.where(even[dim], outer, inner), jnp.where(even[dim], inner, outer)
+
+    rows = [edge(cells, 0, outer) for outer in (False, True)]
+    above, below = sides(0, *[swap(rows[m], (bool(m), None)) for m in range(2)])
+    left, right = sides(1, *[swap(edge(cells, 1, m), (None, m)) for m in (False, True)])
+    corners = [
+        sides(0, *[swap(edge(rows[m], 1, n), (bool(m), n)) for m in range(2)])
+        for n in (False, True)
+    ]
+    top_left, top_right = sides(1, corners[0][0], corners[1][0])
+    bottom_left, bottom_right = sides(1, corners[0][1], corners[1][1])
+    bands = [(top_left, above, top_right), (left, cells, right), (bottom_left, below, bottom_right)]
+    return jnp.concatenate([jnp.concatenate(band, axis=1) for band in bands], axis=0)
 
 
 def call(kernel, name, out_shape, scalars, arrays, scratch):

time: 132 us -> 144 us (1.091)
  the two profiles are of different devices: /device:TPU:6 before, /device:TPU:22 now
where the time goes in v2:
time: 144 us; the launch traced here: 143 us
  Pallas kernels  85.1 us (59%)
  starting transfers between devices  38 us (26%)
  other arithmetic  8.03 us (6%)
  waiting for transfers between devices  7.16 us (5%)
  local copies, waits for them, and re-layouts  4.33 us (3%)
    pallas_call x2, Pallas kernels, call(): pl.pallas_call(kernel, name=name, out_shape=out_shape, in_specs=[pl.Block...  85.1 us
    ppermute x16, starting transfers between devices, swap(): return lax.ppermute(array, axes, pairs)  38 us
    ppermute x16, waiting for transfers between devices, swap(): return lax.ppermute(array, axes, pairs)  7.16 us
    select_n x8, other arithmetic, edge(): return jnp.where(even[dim], *((head, tail) if outer else (tail, head)))  4.33 us
    unnamed x7, local copies, waits for them, and re-layouts  4.33 us
  transfers between devices with their start and end apart: 16, of which 4 were waited for; matrix products, arithmetic and copies ran while one was open for 5% of the time, Pallas kernels for 0%

profile of v2, /device:TPU:22, one launch (start us, length us, event | category | flops | bytes accessed | tf_op | source)
XLA Modules:
  0.0 142.9 jit_solution(4263416852041903842)
XLA Ops:
  0.0 1.3 broadcast_select_fusion.3
  1.3 7.5 %collective-permute-start.4 = (bf16[6,128,256]{2,1,0:T(8,128)(2,1)S(1)}, bf16[6,128,256]{2,1,0:T(8,128)(2,1)S(1)}, u32[]{:S(2)}, u32[]{:S(2)}) collective-permute-start(bf16[6,128,256]{2,1,0:T(8,128)(2,1)S(1)} %get-tuple-element.7), channel_id=1, source_target_pairs={{4,8},{5,9},{6,10},{7,11},{8,4},{9,5},{10,6},{11,7},{12,16},{13,17... | collective-permute-start | bytes 1179656 | tf_op jit(solution)/shard_map/ppermute | solution.py:264
  8.8 1.9 %collective-permute-start.1 = (bf16[6,8,256]{2,1,0:T(8,128)(2,1)S(1)}, bf16[6,8,256]{2,1,0:T(8,128)(2,1)S(1)}, u32[]{:S(2)}, u32[]{:S(2)}) collective-permute-start(bf16[6,8,256]{2,1,0:T(8,128)(2,1)S(1)} %get-tuple-element.24), channel_id=1, source_target_pairs={{1,6},{2,5},{5,2},{6,1},{9,14},{10,13},{13,10},{14,9},{17,22},{18,... | collective-permute-start | bytes 73736 | tf_op jit(solution)/shard_map/ppermute | solution.py:264
  10.7 0.1 collective-permute-start.3
  10.8 4.1 %collective-permute-start = (bf16[6,8,256]{2,1,0:T(8,128)(2,1)S(1)}, bf16[6,8,256]{2,1,0:T(8,128)(2,1)S(1)}, u32[]{:S(2)}, u32[]{:S(2)}) collective-permute-start(bf16[6,8,256]{2,1,0:T(8,128)(2,1)S(1)} %get-tuple-element.22), channel_id=1, source_target_pairs={{5,10},{6,9},{9,6},{10,5},{13,18},{14,17},{17,14},{18,13},{21,26},... | collective-permute-start | bytes 73736 | tf_op jit(solution)/shard_map/ppermute | solution.py:264
  14.9 1.9 %collective-permute-start.2 = (bf16[6,8,256]{2,1,0:T(8,128)(2,1)S(1)}, bf16[6,8,256]{2,1,0:T(8,128)(2,1)S(1)}, u32[]{:S(2)}, u32[]{:S(2)}) collective-permute-start(bf16[6,8,256]{2,1,0:T(8,128)(2,1)S(1)} %get-tuple-element.21), channel_id=1, source_target_pairs={{4,9},{5,8},{6,11},{7,10},{8,5},{9,4},{10,7},{11,6},{12,17},{13,16... | collective-permute-start | bytes 73736 | tf_op jit(solution)/shard_map/ppermute | solution.py:264
  16.8 0.9 broadcast_select_fusion.15
  17.7 0.7 pad_add_fusion.place_ref
  18.4 1.4 %copy.14.taps_ref = bf16[2,49,256]{2,1,0:T(8,128)(2,1)} copy(bf16[2,49,256]{2,0,1:T(2,128)(2,1)} %param.14) | data formatting | bytes 100352 | tf_op args[1]
  19.8 1.5 %copy.16.taps_ref = bf16[2,49,512]{2,1,0:T(8,128)(2,1)} copy(bf16[2,49,512]{2,0,1:T(2,128)(2,1)} %param.18) | data formatting | bytes 200704 | tf_op args[5]
  21.4 1.3 copy.15.marks_ref
  22.7 2.4 %collective-permute-start.6 = (bf16[16,8,256]{2,1,0:T(8,128)(2,1)S(1)}, bf16[16,8,256]{2,1,0:T(8,128)(2,1)S(1)}, u32[]{:S(2)}, u32[]{:S(2)}) collective-permute-start(bf16[16,8,256]{2,1,0:T(8,128)(2,1)S(1)} %get-tuple-element.5), channel_id=1, source_target_pairs={{1,2},{2,1},{5,6},{6,5},{9,10},{10,9},{13,14},{14,13},{17,18},{18,... | collective-permute-start | bytes 196616 | tf_op jit(solution)/shard_map/ppermute | solution.py:264
  25.1 1.4 collective-permute-start.7
  26.5 2.6 %collective-permute-done.6 = bf16[16,8,256]{2,1,0:T(8,128)(2,1)S(1)} collective-permute-done((bf16[16,8,256]{2,1,0:T(8,128)(2,1)S(1)}, bf16[16,8,256]{2,1,0:T(8,128)(2,1)S(1)}, u32[]{:S(2)}, u32[]{:S(2)}) %collective-permute-start.6) | collective-permute-done | bytes 65568 | tf_op jit(solution)/shard_map/ppermute | solution.py:264
  29.1 0.3 collective-permute-done.7
  29.6 1.6 %maximum_maximum_fusion.x_ref = bf16[28,144,256]{2,1,0:T(8,128)(2,1)} fusion(bf16[6,8,256]{2,1,0:T(8,128)(2,1)S(1)} %get-tuple-element.36, bf16[6,128,256]{2,1,0:T(8,128)(2,1)S(1)} %get-tuple-element.12, bf16[6,8,256]{2,1,0:T(8,128)(2,1)S(1)} %get-tuple-element.35, bf16[16,8,256]{2,1,0:T(8,128)(2,1)S(1)} %get-tuple-element.32, ...), kind=kLoop, calls=%fused_computation | loop fusion | flops 18579456 | bytes 4128768 | tf_op jit(solution)/shard_map/concatenate | solution.py:279
  31.2 45.4 %section_one.1 = bf16[8,64,512]{2,1,0:T(8,128)(2,1)} custom-call(s32[2]{0:T(128)} %pad_add_fusion.place_ref, bf16[28,144,256]{2,1,0:T(8,128)(2,1)} %maximum_maximum_fusion.x_ref, bf16[240,144]{1,0:T(8,128)(2,1)} %constant.39.clone.spread_ref, bf16[128,144]{1,0:T(8,128)(2,1)} %constant.40.clone.pick_ref, bf16[2,49,256]{2,1,0:T(8,128)(2,1)} %copy.14.taps_ref, ...), custom_call_target="tpu_custom_call" | custom-call | tf_op jit(solution)/shard_map/section_one/pallas_call | solution.py:283
  76.5 1.3 broadcast_select_fusion.7
  77.8 1.0 collective-permute-start.11
  78.8 3.9 %collective-permute-start.9 = (bf16[6,8,512]{2,1,0:T(8,128)(2,1)S(1)}, bf16[6,8,512]{2,1,0:T(8,128)(2,1)S(1)}, u32[]{:S(2)}, u32[]{:S(2)}) collective-permute-start(bf16[6,8,512]{2,1,0:T(8,128)(2,1)S(1)} %get-tuple-element.20), channel_id=1, source_target_pairs={{1,6},{2,5},{5,2},{6,1},{9,14},{10,13},{13,10},{14,9},{17,22},{18,... | collective-permute-start | bytes 147464 | tf_op jit(solution)/shard_map/ppermute | solution.py:264
  82.7 2.7 %collective-permute-start.10 = (bf16[6,8,512]{2,1,0:T(8,128)(2,1)S(1)}, bf16[6,8,512]{2,1,0:T(8,128)(2,1)S(1)}, u32[]{:S(2)}, u32[]{:S(2)}) collective-permute-start(bf16[6,8,512]{2,1,0:T(8,128)(2,1)S(1)} %get-tuple-element.17), channel_id=1, source_target_pairs={{4,9},{5,8},{6,11},{7,10},{8,5},{9,4},{10,7},{11,6},{12,17},{13,16... | collective-permute-start | bytes 147464 | tf_op jit(solution)/shard_map/ppermute | solution.py:264
  85.4 3.2 %collective-permute-start.8 = (bf16[6,8,512]{2,1,0:T(8,128)(2,1)S(1)}, bf16[6,8,512]{2,1,0:T(8,128)(2,1)S(1)}, u32[]{:S(2)}, u32[]{:S(2)}) collective-permute-start(bf16[6,8,512]{2,1,0:T(8,128)(2,1)S(1)} %get-tuple-element.18), channel_id=1, source_target_pairs={{5,10},{6,9},{9,6},{10,5},{13,18},{14,17},{17,14},{18,13},{21,26},... | collective-permute-start | bytes 147464 | tf_op jit(solution)/shard_map/ppermute | solution.py:264
  88.6 0.9 broadcast_select_fusion.11
  89.5 4.4 %collective-permute-start.12 = (bf16[6,64,512]{2,1,0:T(8,128)(2,1)S(1)}, bf16[6,64,512]{2,1,0:T(8,128)(2,1)S(1)}, u32[]{:S(2)}, u32[]{:S(2)}) collective-permute-start(bf16[6,64,512]{2,1,0:T(8,128)(2,1)S(1)} %get-tuple-element.15), channel_id=1, source_target_pairs={{4,8},{5,9},{6,10},{7,11},{8,4},{9,5},{10,6},{11,7},{12,16},{13,17... | collective-permute-start | bytes 1179656 | tf_op jit(solution)/shard_map/ppermute | solution.py:264
  93.9 0.1 collective-permute-start.13
  94.0 3.5 %collective-permute-start.14 = (bf16[8,8,512]{2,1,0:T(8,128)(2,1)S(1)}, bf16[8,8,512]{2,1,0:T(8,128)(2,1)S(1)}, u32[]{:S(2)}, u32[]{:S(2)}) collective-permute-start(bf16[8,8,512]{2,1,0:T(8,128)(2,1)S(1)} %get-tuple-element.13), channel_id=1, source_target_pairs={{1,2},{2,1},{5,6},{6,5},{9,10},{10,9},{13,14},{14,13},{17,18},{18,... | collective-permute-start | bytes 196616 | tf_op jit(solution)/shard_map/ppermute | solution.py:264
  97.5 0.1 collective-permute-start.15
  97.6 2.7 %collective-permute-done.14 = bf16[8,8,512]{2,1,0:T(8,128)(2,1)S(1)} collective-permute-done((bf16[8,8,512]{2,1,0:T(8,128)(2,1)S(1)}, bf16[8,8,512]{2,1,0:T(8,128)(2,1)S(1)}, u32[]{:S(2)}, u32[]{:S(2)}) %collective-permute-start.14) | collective-permute-done | bytes 65568 | tf_op jit(solution)/shard_map/ppermute | solution.py:264
  100.3 1.5 %collective-permute-done.15 = bf16[8,8,512]{2,1,0:T(8,128)(2,1)S(1)} collective-permute-done((bf16[8,8,512]{2,1,0:T(8,128)(2,1)S(1)}, bf16[8,8,512]{2,1,0:T(8,128)(2,1)S(1)}, u32[]{:S(2)}, u32[]{:S(2)}) %collective-permute-start.15) | collective-permute-done | bytes 65568 | tf_op jit(solution)/shard_map/ppermute | solution.py:264
  101.9 0.1 broadcast_select_fusion.5
  101.9 1.3 maximum_maximum_fusion.1.z_ref
  103.2 39.7 %section_two.1 = bf16[8,64,512]{2,1,0:T(8,128)(2,1)} custom-call(s32[2]{0:T(128)} %pad_add_fusion.place_ref, s32[8,4]{1,0:T(8,128)} %copy.15.marks_ref, bf16[20,80,512]{2,1,0:T(8,128)(2,1)} %maximum_maximum_fusion.1.z_ref, bf16[176,80]{1,0:T(8,128)(2,1)} %constant.41.clone.spread_ref, bf16[64,80]{1,0:T(8,128)(2,1)} %constant.42.clone.pick_ref, ...), custom_call_target="tpu_custom_call" | custom-call | tf_op jit(solution)/shard_map/section_two/pallas_call | solution.py:283
  (26 shorter events, 0.2 us)
Async XLA Ops:
  0.0 29.6 %copy-start.1 = (bf16[16,128,256]{2,1,0:T(8,128)(2,1)S(1)}, bf16[16,128,256]{2,1,0:T(8,128)(2,1)}, u32[]{:S(2)}) copy-start(bf16[16,128,256]{2,1,0:T(8,128)(2,1)} %param.13) | copy-start | bytes 3145732
  1.3 28.2 %collective-permute-start.4 = (bf16[6,128,256]{2,1,0:T(8,128)(2,1)S(1)}, bf16[6,128,256]{2,1,0:T(8,128)(2,1)S(1)}, u32[]{:S(2)}, u32[]{:S(2)}) collective-permute-start(bf16[6,128,256]{2,1,0:T(8,128)(2,1)S(1)} %get-tuple-element.7), channel_id=1, source_target_pairs={{4,8},{5,9},{6,10},{7,11},{8,4},{9,5},{10,6},{11,7},{12,16},{13,17... | collective-permute-start | bytes 1179656 | tf_op jit(solution)/shard_map/ppermute | solution.py:264
  8.8 14.0 %collective-permute-start.1 = (bf16[6,8,256]{2,1,0:T(8,128)(2,1)S(1)}, bf16[6,8,256]{2,1,0:T(8,128)(2,1)S(1)}, u32[]{:S(2)}, u32[]{:S(2)}) collective-permute-start(bf16[6,8,256]{2,1,0:T(8,128)(2,1)S(1)} %get-tuple-element.24), channel_id=1, source_target_pairs={{1,6},{2,5},{5,2},{6,1},{9,14},{10,13},{13,10},{14,9},{17,22},{18,... | collective-permute-start | bytes 73736 | tf_op jit(solution)/shard_map/ppermute | solution.py:264
  10.7 12.0 %collective-permute-start.3 = (bf16[6,8,256]{2,1,0:T(8,128)(2,1)S(1)}, bf16[6,8,256]{2,1,0:T(8,128)(2,1)S(1)}, u32[]{:S(2)}, u32[]{:S(2)}) collective-permute-start(bf16[6,8,256]{2,1,0:T(8,128)(2,1)S(1)} %get-tuple-element.23), channel_id=1, source_target_pairs={{0,5},{1,4},{2,7},{3,6},{4,1},{5,0},{6,3},{7,2},{8,13},{9,12},{10,... | collective-permute-start | bytes 73736 | tf_op jit(solution)/shard_map/ppermute | solution.py:264
  10.8 14.3 %collective-permute-start = (bf16[6,8,256]{2,1,0:T(8,128)(2,1)S(1)}, bf16[6,8,256]{2,1,0:T(8,128)(2,1)S(1)}, u32[]{:S(2)}, u32[]{:S(2)}) collective-permute-start(bf16[6,8,256]{2,1,0:T(8,128)(2,1)S(1)} %get-tuple-element.22), channel_id=1, source_target_pairs={{5,10},{6,9},{9,6},{10,5},{13,18},{14,17},{17,14},{18,13},{21,26},... | collective-permute-start | bytes 73736 | tf_op jit(solution)/shard_map/ppermute | solution.py:264
  14.9 11.6 %collective-permute-start.2 = (bf16[6,8,256]{2,1,0:T(8,128)(2,1)S(1)}, bf16[6,8,256]{2,1,0:T(8,128)(2,1)S(1)}, u32[]{:S(2)}, u32[]{:S(2)}) collective-permute-start(bf16[6,8,256]{2,1,0:T(8,128)(2,1)S(1)} %get-tuple-element.21), channel_id=1, source_target_pairs={{4,9},{5,8},{6,11},{7,10},{8,5},{9,4},{10,7},{11,6},{12,17},{13,16... | collective-permute-start | bytes 73736 | tf_op jit(solution)/shard_map/ppermute | solution.py:264
  22.7 6.8 %collective-permute-start.5 = (bf16[6,128,256]{2,1,0:T(8,128)(2,1)S(1)}, bf16[6,128,256]{2,1,0:T(8,128)(2,1)S(1)}, u32[]{:S(2)}, u32[]{:S(2)}) collective-permute-start(bf16[6,128,256]{2,1,0:T(8,128)(2,1)S(1)} %get-tuple-element.8), channel_id=1, source_target_pairs={{0,4},{1,5},{2,6},{3,7},{4,0},{5,1},{6,2},{7,3},{8,12},{9,13},{10,... | collective-permute-start | bytes 1179656 | tf_op jit(solution)/shard_map/ppermute | solution.py:264
  22.7 6.4 %collective-permute-start.6 = (bf16[16,8,256]{2,1,0:T(8,128)(2,1)S(1)}, bf16[16,8,256]{2,1,0:T(8,128)(2,1)S(1)}, u32[]{:S(2)}, u32[]{:S(2)}) collective-permute-start(bf16[16,8,256]{2,1,0:T(8,128)(2,1)S(1)} %get-tuple-element.5), channel_id=1, source_target_pairs={{1,2},{2,1},{5,6},{6,5},{9,10},{10,9},{13,14},{14,13},{17,18},{18,... | collective-permute-start | bytes 196616 | tf_op jit(solution)/shard_map/ppermute | solution.py:264
  25.1 4.4 %collective-permute-start.7 = (bf16[16,8,256]{2,1,0:T(8,128)(2,1)S(1)}, bf16[16,8,256]{2,1,0:T(8,128)(2,1)S(1)}, u32[]{:S(2)}, u32[]{:S(2)}) collective-permute-start(bf16[16,8,256]{2,1,0:T(8,128)(2,1)S(1)} %get-tuple-element.6), channel_id=1, source_target_pairs={{0,1},{1,0},{2,3},{3,2},{4,5},{5,4},{6,7},{7,6},{8,9},{9,8},{10,11... | collective-permute-start | bytes 196616 | tf_op jit(solution)/shard_map/ppermute | solution.py:264
  76.5 25.4 %copy-start = (bf16[8,64,512]{2,1,0:T(8,128)(2,1)S(1)}, bf16[8,64,512]{2,1,0:T(8,128)(2,1)}, u32[]{:S(2)}) copy-start(bf16[8,64,512]{2,1,0:T(8,128)(2,1)} %section_one.1) | copy-start | bytes 1572868
  77.8 16.0 %collective-permute-start.11 = (bf16[6,8,512]{2,1,0:T(8,128)(2,1)S(1)}, bf16[6,8,512]{2,1,0:T(8,128)(2,1)S(1)}, u32[]{:S(2)}, u32[]{:S(2)}) collective-permute-start(bf16[6,8,512]{2,1,0:T(8,128)(2,1)S(1)} %get-tuple-element.19), channel_id=1, source_target_pairs={{0,5},{1,4},{2,7},{3,6},{4,1},{5,0},{6,3},{7,2},{8,13},{9,12},{10,... | collective-permute-start | bytes 147464 | tf_op jit(solution)/shard_map/ppermute | solution.py:264
  78.8 15.2 %collective-permute-start.9 = (bf16[6,8,512]{2,1,0:T(8,128)(2,1)S(1)}, bf16[6,8,512]{2,1,0:T(8,128)(2,1)S(1)}, u32[]{:S(2)}, u32[]{:S(2)}) collective-permute-start(bf16[6,8,512]{2,1,0:T(8,128)(2,1)S(1)} %get-tuple-element.20), channel_id=1, source_target_pairs={{1,6},{2,5},{5,2},{6,1},{9,14},{10,13},{13,10},{14,9},{17,22},{18,... | collective-permute-start | bytes 147464 | tf_op jit(solution)/shard_map/ppermute | solution.py:264
  82.7 14.8 %collective-permute-start.10 = (bf16[6,8,512]{2,1,0:T(8,128)(2,1)S(1)}, bf16[6,8,512]{2,1,0:T(8,128)(2,1)S(1)}, u32[]{:S(2)}, u32[]{:S(2)}) collective-permute-start(bf16[6,8,512]{2,1,0:T(8,128)(2,1)S(1)} %get-tuple-element.17), channel_id=1, source_target_pairs={{4,9},{5,8},{6,11},{7,10},{8,5},{9,4},{10,7},{11,6},{12,17},{13,16... | collective-permute-start | bytes 147464 | tf_op jit(solution)/shard_map/ppermute | solution.py:264
  85.4 12.2 %collective-permute-start.8 = (bf16[6,8,512]{2,1,0:T(8,128)(2,1)S(1)}, bf16[6,8,512]{2,1,0:T(8,128)(2,1)S(1)}, u32[]{:S(2)}, u32[]{:S(2)}) collective-permute-start(bf16[6,8,512]{2,1,0:T(8,128)(2,1)S(1)} %get-tuple-element.18), channel_id=1, source_target_pairs={{5,10},{6,9},{9,6},{10,5},{13,18},{14,17},{17,14},{18,13},{21,26},... | collective-permute-start | bytes 147464 | tf_op jit(solution)/shard_map/ppermute | solution.py:264
  89.5 12.4 %collective-permute-start.12 = (bf16[6,64,512]{2,1,0:T(8,128)(2,1)S(1)}, bf16[6,64,512]{2,1,0:T(8,128)(2,1)S(1)}, u32[]{:S(2)}, u32[]{:S(2)}) collective-permute-start(bf16[6,64,512]{2,1,0:T(8,128)(2,1)S(1)} %get-tuple-element.15), channel_id=1, source_target_pairs={{4,8},{5,9},{6,10},{7,11},{8,4},{9,5},{10,6},{11,7},{12,16},{13,17... | collective-permute-start | bytes 1179656 | tf_op jit(solution)/shard_map/ppermute | solution.py:264
  93.9 8.0 %collective-permute-start.13 = (bf16[6,64,512]{2,1,0:T(8,128)(2,1)S(1)}, bf16[6,64,512]{2,1,0:T(8,128)(2,1)S(1)}, u32[]{:S(2)}, u32[]{:S(2)}) collective-permute-start(bf16[6,64,512]{2,1,0:T(8,128)(2,1)S(1)} %get-tuple-element.16), channel_id=1, source_target_pairs={{0,4},{1,5},{2,6},{3,7},{4,0},{5,1},{6,2},{7,3},{8,12},{9,13},{10,... | collective-permute-start | bytes 1179656 | tf_op jit(solution)/shard_map/ppermute | solution.py:264
  94.0 6.4 %collective-permute-start.14 = (bf16[8,8,512]{2,1,0:T(8,128)(2,1)S(1)}, bf16[8,8,512]{2,1,0:T(8,128)(2,1)S(1)}, u32[]{:S(2)}, u32[]{:S(2)}) collective-permute-start(bf16[8,8,512]{2,1,0:T(8,128)(2,1)S(1)} %get-tuple-element.13), channel_id=1, source_target_pairs={{1,2},{2,1},{5,6},{6,5},{9,10},{10,9},{13,14},{14,13},{17,18},{18,... | collective-permute-start | bytes 196616 | tf_op jit(solution)/shard_map/ppermute | solution.py:264
  97.5 4.4 %collective-permute-start.15 = (bf16[8,8,512]{2,1,0:T(8,128)(2,1)S(1)}, bf16[8,8,512]{2,1,0:T(8,128)(2,1)S(1)}, u32[]{:S(2)}, u32[]{:S(2)}) collective-permute-start(bf16[8,8,512]{2,1,0:T(8,128)(2,1)S(1)} %get-tuple-element.14), channel_id=1, source_target_pairs={{0,1},{1,0},{2,3},{3,2},{4,5},{5,4},{6,7},{7,6},{8,9},{9,8},{10,11... | collective-permute-start | bytes 196616 | tf_op jit(solution)/shard_map/ppermute | solution.py:264

commit v3 on v1

--- a/solution.py
+++ b/solution.py
@@ -16,6 +16,7 @@
 PAD = 8
 RING = 6
 GROUP = 2
+WIDE_GROUP = 4
 
 
 def spread(width):
@@ -85,7 +86,7 @@
 
 
 def run_block(
-    field_ref, count, group, layer, taps_ref, w_in_ref, w_out_ref, wide, mixed, step, ahead, emit
+    field_ref, count, group, layer, taps_ref, w_in_ref, w_out_ref, wide, mixed, step, ahead, ready, emit
 ):
     planes, depth = field_ref.shape[1] - 6, field_ref.shape[3]
     chunks = depth // 128
@@ -98,12 +99,13 @@
                 mixed[g % 2, c, i] = sums
 
     def project(g):
-        flat = normalize([mixed[g % 2, c] for c in range(chunks)])
+        flat = normalize([mixed[g % 2, c, :group] for c in range(chunks)])
         flat = flat.reshape(group * planes * S, depth)
         branch = mlp(flat, w_in_ref, w_out_ref, layer, step)
         emit(g, branch.reshape(group, planes, S, depth))
 
     mix(0)
+    ready()
 
     def body(g, carry):
         if ahead:
@@ -131,14 +133,27 @@
     return planes * s + t - PAD
 
 
-def permute_rows(spread_ref, source_ref, field_ref, unroll):
+def permute_rows(hot_refs, source_refs, field_ref):
+    spread_ref, middle_ref, sides_ref = hot_refs
+    cells_ref, edges_ref, above_ref, below_ref = source_refs
     shape = field_ref.shape[1:]
-
-    def one(r, carry):
-        field_ref[r] = dot(spread_ref[...], source_ref[r]).astype(BF16).reshape(shape)
+    rows = cells_ref.shape[0]
+
+    def store(r, values):
+        field_ref[r] = values.astype(BF16).reshape(shape)
+
+    def outer(r, carry):
+        store(r, dot(spread_ref[...], above_ref[r]))
+        store(r + RING + rows, dot(spread_ref[...], below_ref[r]))
         return carry
 
-    lax.fori_loop(0, source_ref.shape[0], one, 0, unroll=unroll)
+    def inner(r, carry):
+        values = dot(middle_ref[...], cells_ref[r]) + dot(sides_ref[...], edges_ref[r])
+        store(r + RING, values)
+        return carry
+
+    lax.fori_loop(0, RING, outer, 0, unroll=2)
+    lax.fori_loop(0, rows, inner, 0, unroll=4)
 
 
 def picture_edges(place_ref, ends, columns, rows, cols):
@@ -151,16 +166,31 @@
 
 
 def section_one(
-    ends, place_ref, x_ref, spread_ref, pick_ref, taps_ref, w_in_ref, w_out_ref, stride_ref,
-    out_ref, field0, field1, wide, mixed, patches,
+    ends, place_ref, x_ref, edges_ref, above_ref, below_ref, spread_ref, middle_ref, sides_ref,
+    pick_ref, taps_ref, w_in_hbm, w_out_hbm, stride_hbm,
+    out_ref, field0, field1, wide, mixed, patches, w_in_ref, w_out_ref, stride_ref, arrived,
 ):
-    rows = x_ref.shape[0] - 2 * RING
-    width, depth = x_ref.shape[1:]
+    rows, depth = x_ref.shape[0], x_ref.shape[2]
+    width = spread_ref.shape[1]
     planes = width // S
     pixels = planes * S
+    loads = [
+        pltpu.make_async_copy(source, target, arrived.at[n])
+        for n, (source, target) in enumerate(
+            [(w_in_hbm, w_in_ref), (w_out_hbm, w_out_ref), (stride_hbm, stride_ref)]
+        )
+    ]
+    for load in loads:
+        load.start()
+
+    def ready():
+        for load in loads:
+            load.wait()
+
     columns = column_index(planes)
     top, bottom, inside = picture_edges(place_ref, ends, columns, rows, width - 2 * PAD)
-    permute_rows(spread_ref, x_ref, field0, 4)
+    hot_refs = (spread_ref, middle_ref, sides_ref)
+    permute_rows(hot_refs, (x_ref, edges_ref, above_ref, below_ref), field0)
 
     def first(g, branch):
         for i in range(GROUP):
@@ -170,29 +200,31 @@
             store_planes(field1, at, jnp.where(keep, value, 0.0), planes)
 
     def second(g, branch):
-        for dy in range(2):
-            value = field1[2 * g + dy + 3, 3 : 3 + planes].astype(F32) + branch[dy]
+        for n in range(WIDE_GROUP):
+            dy = n % 2
+            value = field1[WIDE_GROUP * g + n + 3, 3 : 3 + planes].astype(F32) + branch[n]
             value = value.astype(BF16).astype(F32)
             normed = normalize([value[:, :, 128 * c : 128 * c + 128] for c in range(depth // 128)])
             chosen = dot(pick_ref[...], normed.reshape(pixels, depth)).astype(BF16)
             half = chosen.shape[0] // 2
             for dx in range(2):
                 at = (2 * dy + dx) * depth
-                patches[g, :, at : at + depth] = chosen[dx * half : (dx + 1) * half]
-
-    weights = (taps_ref, w_in_ref, w_out_ref, wide, mixed, 256, False)
-    run_block(field0, rows + 6, GROUP, 0, *weights, first)
-    run_block(field1, rows, 2, 1, *weights, second)
+                patches[WIDE_GROUP // 2 * g + n // 2, :, at : at + depth] = chosen[dx * half : (dx + 1) * half]
+
+    weights = (taps_ref, w_in_ref, w_out_ref, wide, mixed, 1024, False)
+    run_block(field0, rows + 6, GROUP, 0, *weights, ready, first)
+    run_block(field1, rows, WIDE_GROUP, 1, *weights, lambda: None, second)
     coarse = dot(patches[...].reshape(-1, 4 * depth), stride_ref[...])
     out_ref[...] = coarse.astype(BF16).reshape(out_ref.shape)
 
 
 def section_two(
-    ends, place_ref, marks_ref, z_ref, spread_ref, pick_ref, taps_ref, w_in_ref, w_out_ref,
-    out_ref, field0, field1, wide, mixed,
+    ends, place_ref, marks_ref, z_ref, edges_ref, above_ref, below_ref, spread_ref, middle_ref,
+    sides_ref, pick_ref, taps_ref, w_in_hbm, w_out_hbm,
+    out_ref, field0, field1, wide, mixed, w_in_ref, w_out_ref, arrived,
 ):
-    rows, cols = out_ref.shape[:2]
-    width, depth = z_ref.shape[1:]
+    rows, cols, depth = z_ref.shape
+    width = spread_ref.shape[1]
     planes = width // S
     pixels = planes * S
 
@@ -205,13 +237,25 @@
 
     @pl.when(jnp.logical_not(clear))
     def _():
-        out_ref[...] = z_ref[RING : RING + rows, PAD : PAD + cols, :]
+        out_ref[...] = z_ref[...]
 
     @pl.when(clear)
     def _():
+        loads = [
+            pltpu.make_async_copy(w_in_hbm, w_in_ref, arrived.at[0]),
+            pltpu.make_async_copy(w_out_hbm, w_out_ref, arrived.at[1]),
+        ]
+        for load in loads:
+            load.start()
+
+        def ready():
+            for load in loads:
+                load.wait()
+
         columns = column_index(planes)
         top, bottom, inside = picture_edges(place_ref, ends, columns, rows, cols)
-        permute_rows(spread_ref, z_ref, field0, 4)
+        hot_refs = (spread_ref, middle_ref, sides_ref)
+        permute_rows(hot_refs, (z_ref, edges_ref, above_ref, below_ref), field0)
 
         def first(g, branch):
             for i in range(GROUP):
@@ -225,82 +269,90 @@
                 store_planes(field1, at, jnp.where(keep, new, 0.0), planes)
 
         def second(g, branch):
-            for i in range(2):
-                at = 2 * g + i
+            for i in range(GROUP):
+                at = GROUP * g + i
                 new = field1[at + 3, 3 : 3 + planes].astype(F32) + branch[i]
                 new = new.astype(BF16).reshape(pixels, depth)
                 out_ref[at] = dot(pick_ref[...], new).astype(BF16)
 
-        weights = (taps_ref, w_in_ref, w_out_ref, wide, mixed, 512, True)
-        run_block(field0, rows + 6, GROUP, 0, *weights, first)
-        run_block(field1, rows, 2, 1, *weights, second)
-
-
-def with_halo(cells):
-    for axis, dim, width in (("col", 1, PAD), ("row", 0, RING)):
+        weights = (taps_ref, w_in_ref, w_out_ref, wide, mixed, 1024, True)
+        run_block(field0, rows + 6, GROUP, 0, *weights, ready, first)
+        run_block(field1, rows, GROUP, 1, *weights, lambda: None, second)
+
+
+def halo(cells):
+    def swap(axis, head, tail):
         count = lax.axis_size(axis)
         even = lax.axis_index(axis) % 2 == 0
-        head = lax.slice_in_dim(cells, 0, width, axis=dim)
-        tail = lax.slice_in_dim(cells, cells.shape[dim] - width, cells.shape[dim], axis=dim)
         inner = [(i, i ^ 1) for i in range(count)]
         outer = [(i, (i - 1 ^ 1) + 1) for i in range(1, count - 1)]
         near = lax.ppermute(jnp.where(even, tail, head), axis, inner)
         far = lax.ppermute(jnp.where(even, head, tail), axis, outer)
-        before = jnp.where(even, far, near)
-        after = jnp.where(even, near, far)
-        cells = jnp.concatenate([before, cells, after], axis=dim)
-    return cells
-
-
-def call(kernel, name, out_shape, scalars, arrays, scratch):
+        return jnp.where(even, far, near), jnp.where(even, near, far)
+
+    left, right = swap("col", cells[:, :PAD], cells[:, -PAD:])
+
+    def band(rows):
+        return jnp.concatenate([left[rows], cells[rows], right[rows]], axis=1)
+
+    above, below = swap("row", band(slice(0, RING)), band(slice(-RING, None)))
+    return [cells, jnp.concatenate([left, right], axis=1), above, below]
+
+
+def call(kernel, name, out_shape, scalars, arrays, weights, scratch):
+    spaces = [pltpu.SMEM] * len(scalars) + [pltpu.VMEM] * len(arrays) + [pl.ANY] * len(weights)
+    buffers = scratch + [(w.shape, w.dtype) for w in weights]
     return pl.pallas_call(
         kernel,
         name=name,
         out_shape=out_shape,
-        in_specs=[pl.BlockSpec(memory_space=pltpu.SMEM) for _ in scalars]
-        + [pl.BlockSpec(memory_space=pltpu.VMEM) for _ in arrays],
+        in_specs=[pl.BlockSpec(memory_space=space) for space in spaces],
         out_specs=pl.BlockSpec(memory_space=pltpu.VMEM),
-        scratch_shapes=[pltpu.VMEM(shape, dtype) for shape, dtype in scratch],
+        scratch_shapes=[pltpu.VMEM(shape, dtype) for shape, dtype in buffers]
+        + [pltpu.SemaphoreType.DMA((len(weights),))],
         compiler_params=pltpu.CompilerParams(vmem_limit_bytes=56 * 1024 * 1024),
-    )(*scalars, *arrays)
-
-
-def run_one(ends, place, padded, taps, w_in, w_out, stride):
-    rows, width, depth = padded.shape
-    rows -= 2 * RING
-    planes = width // S
-    half = (width - 2 * PAD) // 2
-    wide_depth = stride.shape[1]
-    columns = [2 * j + dx for dx in range(2) for j in range(half)]
+    )(*scalars, *arrays, *weights)
+
+
+def one_hots(width, columns):
+    hot = spread(width)
+    sides = np.concatenate([hot[:, :PAD], hot[:, -PAD:]], axis=1)
+    return [jnp.asarray(m, BF16) for m in (hot, hot[:, PAD:-PAD], sides, pick(width, columns))]
+
+
+def run_one(ends, place, sources, taps, w_in, w_out, stride):
+    rows, cols, depth = sources[0].shape
+    width = cols + 2 * PAD
+    planes = width // S
+    columns = [2 * j + dx for dx in range(2) for j in range(cols // 2)]
     return call(
         functools.partial(section_one, ends),
         "section_one",
-        jax.ShapeDtypeStruct((rows // 2, half, wide_depth), BF16),
+        jax.ShapeDtypeStruct((rows // 2, cols // 2, stride.shape[1]), BF16),
         [place],
-        [padded, jnp.asarray(spread(width), BF16), jnp.asarray(pick(width, columns), BF16),
-         taps, w_in, w_out, stride],
+        [*sources, *one_hots(width, columns), taps],
+        [w_in, w_out, stride],
         [
             ((rows + 2 * RING, planes + 6, S, depth), BF16),
             ((rows + 6, planes + 6, S, depth), BF16),
             ((49, 8, depth), F32),
-            ((2, depth // 128, GROUP, planes, S, 128), F32),
-            ((rows // 2, half, 4 * depth), BF16),
+            ((2, depth // 128, WIDE_GROUP, planes, S, 128), F32),
+            ((rows // 2, cols // 2, 4 * depth), BF16),
         ],
     )
 
 
-def run_two(ends, place, marks, padded, taps, w_in, w_out):
-    rows, width, depth = padded.shape
-    rows -= 2 * RING
-    cols = width - 2 * PAD
+def run_two(ends, place, marks, sources, taps, w_in, w_out):
+    rows, cols, depth = sources[0].shape
+    width = cols + 2 * PAD
     planes = width // S
     return call(
         functools.partial(section_two, ends),
         "section_two",
         jax.ShapeDtypeStruct((rows, cols, depth), BF16),
         [place, marks],
-        [padded, jnp.asarray(spread(width), BF16), jnp.asarray(pick(width, range(cols)), BF16),
-         taps, w_in, w_out],
+        [*sources, *one_hots(width, range(cols)), taps],
+        [w_in, w_out],
         [
             ((rows + 2 * RING, planes + 6, S, depth), BF16),
             ((rows + 6, planes + 6, S, depth), BF16),
@@ -327,7 +379,7 @@
     coarse = run_one(
         ends,
         place,
-        with_halo(input_picture),
+        halo(input_picture),
         spatial_taps_first,
         widening_matrix_first,
         narrowing_matrix_first,
@@ -337,7 +389,7 @@
         ends,
         place,
         sky_clarity_marks,
-        with_halo(coarse),
+        halo(coarse),
         spatial_taps_second,
         widening_matrix_second,
         narrowing_matrix_second,

time: 132 us -> 121 us (0.917)
  the two profiles are of different devices: /device:TPU:6 before, /device:TPU:20 now
where the time goes in v3:
time: 121 us; the launch traced here: 120 us
  Pallas kernels  77.1 us (64%)
  starting transfers between devices  16.3 us (13%)
  waiting for transfers between devices  15.2 us (13%)
  other arithmetic  6.09 us (5%)
  local copies, waits for them, and re-layouts  5.14 us (4%)
    pallas_call x2, Pallas kernels, call(): pl.pallas_call(kernel, name=name, out_shape=out_shape, in_specs=[pl.Block...  77.1 us
    ppermute x4, starting transfers between devices, swap(): far = lax.ppermute(jnp.where(even, head, tail), axis, outer)  15.9 us
    ppermute x4, waiting for transfers between devices, swap(): far = lax.ppermute(jnp.where(even, head, tail), axis, outer)  12.9 us
    unnamed x7, local copies, waits for them, and re-layouts  2.76 us
  transfers between devices with their start and end apart: 8, of which 6 were waited for; matrix products, arithmetic and copies ran while one was open for 6% of the time, Pallas kernels for 0%

profile of v3, /device:TPU:20, one launch (start us, length us, event | category | flops | bytes accessed | tf_op | source)
XLA Modules:
  0.0 120.2 jit_solution(13874814329941480339)
XLA Ops:
  0.0 0.9 broadcast_select_fusion.15
  0.9 2.4 %collective-permute-start = (bf16[16,8,256]{2,1,0:T(8,128)(2,1)S(1)}, bf16[16,8,256]{2,1,0:T(8,128)(2,1)S(1)}, u32[]{:S(2)}, u32[]{:S(2)}) collective-permute-start(bf16[16,8,256]{2,1,0:T(8,128)(2,1)S(1)} %get-tuple-element.7), channel_id=1, source_target_pairs={{1,2},{2,1},{5,6},{6,5},{9,10},{10,9},{13,14},{14,13},{17,18},{18,... | collective-permute-start | bytes 196616 | tf_op jit(solution)/shard_map/ppermute | solution.py:290
  3.3 0.1 collective-permute-start.1
  3.4 1.2 fusion
  4.5 2.5 %collective-permute-done = bf16[16,8,256]{2,1,0:T(8,128)(2,1)S(1)} collective-permute-done((bf16[16,8,256]{2,1,0:T(8,128)(2,1)S(1)}, bf16[16,8,256]{2,1,0:T(8,128)(2,1)S(1)}, u32[]{:S(2)}, u32[]{:S(2)}) %collective-permute-start) | collective-permute-done | bytes 65568 | tf_op jit(solution)/shard_map/ppermute | solution.py:290
  7.0 0.6 collective-permute-done.1
  7.6 0.2 broadcast_select_fusion.6
  7.8 5.7 %collective-permute-start.2 = (bf16[6,144,256]{2,1,0:T(8,128)(2,1)S(1)}, bf16[6,144,256]{2,1,0:T(8,128)(2,1)S(1)}, u32[]{:S(2)}, u32[]{:S(2)}) collective-permute-start(bf16[6,144,256]{2,1,0:T(8,128)(2,1)S(1)} %get-tuple-element.16), channel_id=1, source_target_pairs={{4,8},{8,4},{12,16},{16,12},{20,24},{24,20},{28,32},{32,28},{36,40... | collective-permute-start | bytes 1327112 | tf_op jit(solution)/shard_map/ppermute | solution.py:290
  13.6 0.1 collective-permute-start.3
  13.7 1.4 %copy.18.taps_ref = bf16[2,49,256]{2,1,0:T(8,128)(2,1)} copy(bf16[2,49,256]{2,0,1:T(2,128)(2,1)} %param.18) | data formatting | bytes 100352 | tf_op args[1]
  15.1 0.6 pad_add_fusion.place_ref
  15.7 0.7 pad_maximum_fusion.4.edges_ref
  16.3 3.2 %collective-permute-done.2 = bf16[6,144,256]{2,1,0:T(8,128)(2,1)S(1)} collective-permute-done((bf16[6,144,256]{2,1,0:T(8,128)(2,1)S(1)}, bf16[6,144,256]{2,1,0:T(8,128)(2,1)S(1)}, u32[]{:S(2)}, u32[]{:S(2)}) %collective-permute-start.2) | collective-permute-done | bytes 442400 | tf_op jit(solution)/shard_map/ppermute | solution.py:290
  19.5 0.0 collective-permute-done.3
  19.6 1.0 broadcast_select_fusion.4
  20.5 43.1 %section_one.1.z_ref = bf16[8,64,512]{2,1,0:T(8,128)(2,1)} custom-call(s32[2]{0:T(128)} %pad_add_fusion.place_ref, bf16[16,128,256]{2,1,0:T(8,128)(2,1)} %x_ref.1, bf16[16,16,256]{2,1,0:T(8,128)(2,1)} %pad_maximum_fusion.4.edges_ref, bf16[6,144,256]{2,1,0:T(8,128)(2,1)} %get-tuple-element.14.above_ref, bf16[6,144,256]{2,1,0:T(8,128)(2,1)} %get-tuple-element.13.below_ref, ...), custom_call_target="tpu_custom_call" | custom-call | tf_op jit(solution)/shard_map/section_one/pallas_call | solution.py:305
  63.7 0.9 broadcast_select_fusion.11
  64.6 3.5 %collective-permute-start.4 = (bf16[8,8,512]{2,1,0:T(8,128)(2,1)S(1)}, bf16[8,8,512]{2,1,0:T(8,128)(2,1)S(1)}, u32[]{:S(2)}, u32[]{:S(2)}) collective-permute-start(bf16[8,8,512]{2,1,0:T(8,128)(2,1)S(1)} %get-tuple-element.19), channel_id=1, source_target_pairs={{1,2},{2,1},{5,6},{6,5},{9,10},{10,9},{13,14},{14,13},{17,18},{18,... | collective-permute-start | bytes 196616 | tf_op jit(solution)/shard_map/ppermute | solution.py:290
  68.1 0.1 collective-permute-start.5
  68.2 1.2 fusion.1
  69.4 1.4 %collective-permute-done.4 = bf16[8,8,512]{2,1,0:T(8,128)(2,1)S(1)} collective-permute-done((bf16[8,8,512]{2,1,0:T(8,128)(2,1)S(1)}, bf16[8,8,512]{2,1,0:T(8,128)(2,1)S(1)}, u32[]{:S(2)}, u32[]{:S(2)}) %collective-permute-start.4) | collective-permute-done | bytes 65568 | tf_op jit(solution)/shard_map/ppermute | solution.py:290
  70.7 1.7 %collective-permute-done.5 = bf16[8,8,512]{2,1,0:T(8,128)(2,1)S(1)} collective-permute-done((bf16[8,8,512]{2,1,0:T(8,128)(2,1)S(1)}, bf16[8,8,512]{2,1,0:T(8,128)(2,1)S(1)}, u32[]{:S(2)}, u32[]{:S(2)}) %collective-permute-start.5) | collective-permute-done | bytes 65568 | tf_op jit(solution)/shard_map/ppermute | solution.py:289
  72.5 0.2 broadcast_select_fusion.2
  72.7 4.3 %collective-permute-start.6 = (bf16[6,80,512]{2,1,0:T(8,128)(2,1)S(1)}, bf16[6,80,512]{2,1,0:T(8,128)(2,1)S(1)}, u32[]{:S(2)}, u32[]{:S(2)}) collective-permute-start(bf16[6,80,512]{2,1,0:T(8,128)(2,1)S(1)} %get-tuple-element.12), channel_id=1, source_target_pairs={{4,8},{8,4},{12,16},{16,12},{20,24},{24,20},{28,32},{32,28},{36,40... | collective-permute-start | bytes 1474568 | tf_op jit(solution)/shard_map/ppermute | solution.py:290
  77.0 0.1 collective-permute-start.7
  77.2 0.6 copy.20.taps_ref
  77.8 0.7 copy.19.marks_ref
  78.5 0.7 pad_maximum_fusion.5.edges_ref
  79.1 5.8 %collective-permute-done.6 = bf16[6,80,512]{2,1,0:T(8,128)(2,1)S(1)} collective-permute-done((bf16[6,80,512]{2,1,0:T(8,128)(2,1)S(1)}, bf16[6,80,512]{2,1,0:T(8,128)(2,1)S(1)}, u32[]{:S(2)}, u32[]{:S(2)}) %collective-permute-start.6) | collective-permute-done | bytes 491552 | tf_op jit(solution)/shard_map/ppermute | solution.py:290
  85.0 0.0 collective-permute-done.7
  85.0 1.0 broadcast_select_fusion
  86.0 34.0 %section_two.1 = bf16[8,64,512]{2,1,0:T(8,128)(2,1)} custom-call(s32[2]{0:T(128)} %pad_add_fusion.place_ref, s32[8,4]{1,0:T(8,128)} %copy.19.marks_ref, bf16[8,64,512]{2,1,0:T(8,128)(2,1)} %section_one.1.z_ref, bf16[8,16,512]{2,1,0:T(8,128)(2,1)} %pad_maximum_fusion.5.edges_ref, bf16[6,80,512]{2,1,0:T(8,128)(2,1)} %get-tuple-element.10.above_ref, ...), custom_call_target="tpu_custom_call" | custom-call | tf_op jit(solution)/shard_map/section_two/pallas_call | solution.py:305
  (9 shorter events, 0.1 us)
Async XLA Ops:
  0.9 6.2 %collective-permute-start = (bf16[16,8,256]{2,1,0:T(8,128)(2,1)S(1)}, bf16[16,8,256]{2,1,0:T(8,128)(2,1)S(1)}, u32[]{:S(2)}, u32[]{:S(2)}) collective-permute-start(bf16[16,8,256]{2,1,0:T(8,128)(2,1)S(1)} %get-tuple-element.7), channel_id=1, source_target_pairs={{1,2},{2,1},{5,6},{6,5},{9,10},{10,9},{13,14},{14,13},{17,18},{18,... | collective-permute-start | bytes 196616 | tf_op jit(solution)/shard_map/ppermute | solution.py:290
  3.3 4.4 %collective-permute-start.1 = (bf16[16,8,256]{2,1,0:T(8,128)(2,1)S(1)}, bf16[16,8,256]{2,1,0:T(8,128)(2,1)S(1)}, u32[]{:S(2)}, u32[]{:S(2)}) collective-permute-start(bf16[16,8,256]{2,1,0:T(8,128)(2,1)S(1)} %get-tuple-element.8), channel_id=1, source_target_pairs={{0,1},{1,0},{2,3},{3,2},{4,5},{5,4},{6,7},{7,6},{8,9},{9,8},{10,11... | collective-permute-start | bytes 196616 | tf_op jit(solution)/shard_map/ppermute | solution.py:289
  7.8 11.7 %collective-permute-start.2 = (bf16[6,144,256]{2,1,0:T(8,128)(2,1)S(1)}, bf16[6,144,256]{2,1,0:T(8,128)(2,1)S(1)}, u32[]{:S(2)}, u32[]{:S(2)}) collective-permute-start(bf16[6,144,256]{2,1,0:T(8,128)(2,1)S(1)} %get-tuple-element.16), channel_id=1, source_target_pairs={{4,8},{8,4},{12,16},{16,12},{20,24},{24,20},{28,32},{32,28},{36,40... | collective-permute-start | bytes 1327112 | tf_op jit(solution)/shard_map/ppermute | solution.py:290
  13.6 6.0 %collective-permute-start.3 = (bf16[6,144,256]{2,1,0:T(8,128)(2,1)S(1)}, bf16[6,144,256]{2,1,0:T(8,128)(2,1)S(1)}, u32[]{:S(2)}, u32[]{:S(2)}) collective-permute-start(bf16[6,144,256]{2,1,0:T(8,128)(2,1)S(1)} %get-tuple-element.15), channel_id=1, source_target_pairs={{0,4},{4,0},{8,12},{12,8},{16,20},{20,16},{24,28},{28,24},{32,36},... | collective-permute-start | bytes 1327112 | tf_op jit(solution)/shard_map/ppermute | solution.py:289
  20.5 56.6 %copy-start = (bf16[2,49,512]{2,0,1:T(2,128)(2,1)S(1)}, bf16[2,49,512]{2,0,1:T(2,128)(2,1)}, u32[]{:S(2)}) copy-start(bf16[2,49,512]{2,0,1:T(2,128)(2,1)} %param.22) | copy-start | bytes 301060
  20.5 57.3 %copy-start.1 = (s32[8,4]{0,1:T(4,128)S(1)}, s32[8,4]{0,1:T(4,128)}, u32[]{:S(2)}) copy-start(s32[8,4]{0,1:T(4,128)} %param.25) | copy-start | bytes 388
  64.6 6.2 %collective-permute-start.4 = (bf16[8,8,512]{2,1,0:T(8,128)(2,1)S(1)}, bf16[8,8,512]{2,1,0:T(8,128)(2,1)S(1)}, u32[]{:S(2)}, u32[]{:S(2)}) collective-permute-start(bf16[8,8,512]{2,1,0:T(8,128)(2,1)S(1)} %get-tuple-element.19), channel_id=1, source_target_pairs={{1,2},{2,1},{5,6},{6,5},{9,10},{10,9},{13,14},{14,13},{17,18},{18,... | collective-permute-start | bytes 196616 | tf_op jit(solution)/shard_map/ppermute | solution.py:290
  68.1 4.4 %collective-permute-start.5 = (bf16[8,8,512]{2,1,0:T(8,128)(2,1)S(1)}, bf16[8,8,512]{2,1,0:T(8,128)(2,1)S(1)}, u32[]{:S(2)}, u32[]{:S(2)}) collective-permute-start(bf16[8,8,512]{2,1,0:T(8,128)(2,1)S(1)} %get-tuple-element.20), channel_id=1, source_target_pairs={{0,1},{1,0},{2,3},{3,2},{4,5},{5,4},{6,7},{7,6},{8,9},{9,8},{10,11... | collective-permute-start | bytes 196616 | tf_op jit(solution)/shard_map/ppermute | solution.py:289
  72.7 12.3 %collective-permute-start.6 = (bf16[6,80,512]{2,1,0:T(8,128)(2,1)S(1)}, bf16[6,80,512]{2,1,0:T(8,128)(2,1)S(1)}, u32[]{:S(2)}, u32[]{:S(2)}) collective-permute-start(bf16[6,80,512]{2,1,0:T(8,128)(2,1)S(1)} %get-tuple-element.12), channel_id=1, source_target_pairs={{4,8},{8,4},{12,16},{16,12},{20,24},{24,20},{28,32},{32,28},{36,40... | collective-permute-start | bytes 1474568 | tf_op jit(solution)/shard_map/ppermute | solution.py:290
  77.0 7.9 %collective-permute-start.7 = (bf16[6,80,512]{2,1,0:T(8,128)(2,1)S(1)}, bf16[6,80,512]{2,1,0:T(8,128)(2,1)S(1)}, u32[]{:S(2)}, u32[]{:S(2)}) collective-permute-start(bf16[6,80,512]{2,1,0:T(8,128)(2,1)S(1)} %get-tuple-element.11), channel_id=1, source_target_pairs={{0,4},{4,0},{8,12},{12,8},{16,20},{20,16},{24,28},{28,24},{32,36},... | collective-permute-start | bytes 1474568 | tf_op jit(solution)/shard_map/ppermute | solution.py:289

commit v4 on v3

--- a/solution.py
+++ b/solution.py
@@ -133,18 +133,20 @@
     return planes * s + t - PAD
 
 
-def permute_rows(hot_refs, source_refs, field_ref):
+def permute_rows(place_ref, hot_refs, source_refs, field_ref):
     spread_ref, middle_ref, sides_ref = hot_refs
-    cells_ref, edges_ref, above_ref, below_ref = source_refs
+    cells_ref, edges_ref, near_ref, far_ref = source_refs
     shape = field_ref.shape[1:]
     rows = cells_ref.shape[0]
+    odd = place_ref[0] % 2
+    below = RING + rows
 
     def store(r, values):
         field_ref[r] = values.astype(BF16).reshape(shape)
 
     def outer(r, carry):
-        store(r, dot(spread_ref[...], above_ref[r]))
-        store(r + RING + rows, dot(spread_ref[...], below_ref[r]))
+        store(r + below * (1 - odd), dot(spread_ref[...], near_ref[r]))
+        store(r + below * odd, dot(spread_ref[...], far_ref[r]))
         return carry
 
     def inner(r, carry):
@@ -166,7 +168,7 @@
 
 
 def section_one(
-    ends, place_ref, x_ref, edges_ref, above_ref, below_ref, spread_ref, middle_ref, sides_ref,
+    ends, place_ref, x_ref, edges_ref, near_ref, far_ref, spread_ref, middle_ref, sides_ref,
     pick_ref, taps_ref, w_in_hbm, w_out_hbm, stride_hbm,
     out_ref, field0, field1, wide, mixed, patches, w_in_ref, w_out_ref, stride_ref, arrived,
 ):
@@ -190,7 +192,7 @@
     columns = column_index(planes)
     top, bottom, inside = picture_edges(place_ref, ends, columns, rows, width - 2 * PAD)
     hot_refs = (spread_ref, middle_ref, sides_ref)
-    permute_rows(hot_refs, (x_ref, edges_ref, above_ref, below_ref), field0)
+    permute_rows(place_ref, hot_refs, (x_ref, edges_ref, near_ref, far_ref), field0)
 
     def first(g, branch):
         for i in range(GROUP):
@@ -219,7 +221,7 @@
 
 
 def section_two(
-    ends, place_ref, marks_ref, z_ref, edges_ref, above_ref, below_ref, spread_ref, middle_ref,
+    ends, place_ref, marks_ref, z_ref, edges_ref, near_ref, far_ref, spread_ref, middle_ref,
     sides_ref, pick_ref, taps_ref, w_in_hbm, w_out_hbm,
     out_ref, field0, field1, wide, mixed, w_in_ref, w_out_ref, arrived,
 ):
@@ -255,7 +257,7 @@
         columns = column_index(planes)
         top, bottom, inside = picture_edges(place_ref, ends, columns, rows, cols)
         hot_refs = (spread_ref, middle_ref, sides_ref)
-        permute_rows(hot_refs, (z_ref, edges_ref, above_ref, below_ref), field0)
+        permute_rows(place_ref, hot_refs, (z_ref, edges_ref, near_ref, far_ref), field0)
 
         def first(g, branch):
             for i in range(GROUP):
@@ -288,15 +290,16 @@
         outer = [(i, (i - 1 ^ 1) + 1) for i in range(1, count - 1)]
         near = lax.ppermute(jnp.where(even, tail, head), axis, inner)
         far = lax.ppermute(jnp.where(even, head, tail), axis, outer)
-        return jnp.where(even, far, near), jnp.where(even, near, far)
-
-    left, right = swap("col", cells[:, :PAD], cells[:, -PAD:])
+        return even, near, far
+
+    even, near, far = swap("col", cells[:, :PAD], cells[:, -PAD:])
+    left, right = jnp.where(even, far, near), jnp.where(even, near, far)
 
     def band(rows):
         return jnp.concatenate([left[rows], cells[rows], right[rows]], axis=1)
 
-    above, below = swap("row", band(slice(0, RING)), band(slice(-RING, None)))
-    return [cells, jnp.concatenate([left, right], axis=1), above, below]
+    _, near, far = swap("row", band(slice(0, RING)), band(slice(-RING, None)))
+    return [cells, jnp.concatenate([left, right], axis=1), near, far]
 
 
 def call(kernel, name, out_shape, scalars, arrays, weights, scratch):

time: 121 us -> 123 us (1.017)
  the two profiles are of different devices: /device:TPU:20 before, /device:TPU:22 now
where the time goes in v4:
time: 123 us; the launch traced here: 122 us
  Pallas kernels  77.1 us (63%)
  starting transfers between devices  18.7 us (15%)
  waiting for transfers between devices  15.3 us (12%)
  local copies, waits for them, and re-layouts  6.73 us (5%)
  other arithmetic  4.11 us (3%)
    pallas_call x2, Pallas kernels, call(): pl.pallas_call(kernel, name=name, out_shape=out_shape, in_specs=[pl.Block...  77.1 us
    ppermute x4, starting transfers between devices, swap(): far = lax.ppermute(jnp.where(even, head, tail), axis, outer)  18.3 us
    ppermute x4, waiting for transfers between devices, swap(): far = lax.ppermute(jnp.where(even, head, tail), axis, outer)  13 us
    unnamed x15, local copies, waits for them, and re-layouts  4.34 us
  transfers between devices with their start and end apart: 8, of which 6 were waited for; matrix products, arithmetic and copies ran while one was open for 6% of the time, Pallas kernels for 0%

profile of v4, /device:TPU:22, one launch (start us, length us, event | category | flops | bytes accessed | tf_op | source)
XLA Modules:
  0.0 122.2 jit_solution(14684062881115384005)
XLA Ops:
  0.0 0.9 broadcast_select_fusion.11
  0.9 2.4 %collective-permute-start = (bf16[16,8,256]{2,1,0:T(8,128)(2,1)S(1)}, bf16[16,8,256]{2,1,0:T(8,128)(2,1)S(1)}, u32[]{:S(2)}, u32[]{:S(2)}) collective-permute-start(bf16[16,8,256]{2,1,0:T(8,128)(2,1)S(1)} %get-tuple-element.7), channel_id=1, source_target_pairs={{1,2},{2,1},{5,6},{6,5},{9,10},{10,9},{13,14},{14,13},{17,18},{18,... | collective-permute-start | bytes 196616 | tf_op jit(solution)/shard_map/ppermute | solution.py:292
  3.3 0.1 collective-permute-start.1
  3.4 1.2 fusion
  4.5 2.5 %collective-permute-done = bf16[16,8,256]{2,1,0:T(8,128)(2,1)S(1)} collective-permute-done((bf16[16,8,256]{2,1,0:T(8,128)(2,1)S(1)}, bf16[16,8,256]{2,1,0:T(8,128)(2,1)S(1)}, u32[]{:S(2)}, u32[]{:S(2)}) %collective-permute-start) | collective-permute-done | bytes 65568 | tf_op jit(solution)/shard_map/ppermute | solution.py:292
  7.0 0.6 collective-permute-done.1
  7.6 0.2 broadcast_select_fusion.2
  7.8 0.1 collective-permute-start.2
  7.9 8.1 %collective-permute-start.3 = (bf16[6,144,256]{2,1,0:T(8,128)(2,1)S(1)}, bf16[6,144,256]{2,1,0:T(8,128)(2,1)S(1)}, u32[]{:S(2)}, u32[]{:S(2)}) collective-permute-start(bf16[6,144,256]{2,1,0:T(8,128)(2,1)S(1)} %get-tuple-element.11), channel_id=1, source_target_pairs={{4,8},{8,4},{12,16},{16,12},{20,24},{24,20},{28,32},{32,28},{36,40... | collective-permute-start | bytes 1327112 | tf_op jit(solution)/shard_map/ppermute | solution.py:292
  16.0 1.4 %copy.18.taps_ref = bf16[2,49,256]{2,1,0:T(8,128)(2,1)} copy(bf16[2,49,256]{2,0,1:T(2,128)(2,1)} %param.18) | data formatting | bytes 100352 | tf_op args[1]
  17.5 0.6 pad_add_fusion.place_ref
  18.1 0.7 pad_maximum_fusion.4.edges_ref
  18.7 0.0 collective-permute-done.2.near_ref
  18.7 3.3 %collective-permute-done.3.far_ref = bf16[6,144,256]{2,1,0:T(8,128)(2,1)S(1)} collective-permute-done((bf16[6,144,256]{2,1,0:T(8,128)(2,1)S(1)}, bf16[6,144,256]{2,1,0:T(8,128)(2,1)S(1)}, u32[]{:S(2)}, u32[]{:S(2)}) %collective-permute-start.3) | collective-permute-done | bytes 442400 | tf_op jit(solution)/shard_map/ppermute | solution.py:292
  22.0 0.8 copy-done.3
  22.8 43.1 %section_one.1.z_ref = bf16[8,64,512]{2,1,0:T(8,128)(2,1)} custom-call(s32[2]{0:T(128)} %pad_add_fusion.place_ref, bf16[16,128,256]{2,1,0:T(8,128)(2,1)} %x_ref.1, bf16[16,16,256]{2,1,0:T(8,128)(2,1)} %pad_maximum_fusion.4.edges_ref, bf16[6,144,256]{2,1,0:T(8,128)(2,1)} %copy-done.2, bf16[6,144,256]{2,1,0:T(8,128)(2,1)} %copy-done.3, ...), custom_call_target="tpu_custom_call" | custom-call | tf_op jit(solution)/shard_map/section_one/pallas_call | solution.py:308
  65.9 0.9 broadcast_select_fusion.7
  66.8 3.5 %collective-permute-start.4 = (bf16[8,8,512]{2,1,0:T(8,128)(2,1)S(1)}, bf16[8,8,512]{2,1,0:T(8,128)(2,1)S(1)}, u32[]{:S(2)}, u32[]{:S(2)}) collective-permute-start(bf16[8,8,512]{2,1,0:T(8,128)(2,1)S(1)} %get-tuple-element.15), channel_id=1, source_target_pairs={{1,2},{2,1},{5,6},{6,5},{9,10},{10,9},{13,14},{14,13},{17,18},{18,... | collective-permute-start | bytes 196616 | tf_op jit(solution)/shard_map/ppermute | solution.py:292
  70.3 0.1 collective-permute-start.5
  70.4 1.2 fusion.1
  71.6 1.4 %collective-permute-done.4 = bf16[8,8,512]{2,1,0:T(8,128)(2,1)S(1)} collective-permute-done((bf16[8,8,512]{2,1,0:T(8,128)(2,1)S(1)}, bf16[8,8,512]{2,1,0:T(8,128)(2,1)S(1)}, u32[]{:S(2)}, u32[]{:S(2)}) %collective-permute-start.4) | collective-permute-done | bytes 65568 | tf_op jit(solution)/shard_map/ppermute | solution.py:292
  73.0 1.7 %collective-permute-done.5 = bf16[8,8,512]{2,1,0:T(8,128)(2,1)S(1)} collective-permute-done((bf16[8,8,512]{2,1,0:T(8,128)(2,1)S(1)}, bf16[8,8,512]{2,1,0:T(8,128)(2,1)S(1)}, u32[]{:S(2)}, u32[]{:S(2)}) %collective-permute-start.5) | collective-permute-done | bytes 65568 | tf_op jit(solution)/shard_map/ppermute | solution.py:291
  74.7 0.2 broadcast_select_fusion
  74.9 0.1 collective-permute-start.6
  75.0 4.3 %collective-permute-start.7 = (bf16[6,80,512]{2,1,0:T(8,128)(2,1)S(1)}, bf16[6,80,512]{2,1,0:T(8,128)(2,1)S(1)}, u32[]{:S(2)}, u32[]{:S(2)}) collective-permute-start(bf16[6,80,512]{2,1,0:T(8,128)(2,1)S(1)} %get-tuple-element.9), channel_id=1, source_target_pairs={{4,8},{8,4},{12,16},{16,12},{20,24},{24,20},{28,32},{32,28},{36,40... | collective-permute-start | bytes 1474568 | tf_op jit(solution)/shard_map/ppermute | solution.py:292
  79.4 0.7 copy.20.taps_ref
  80.0 0.7 copy.19.marks_ref
  80.7 0.7 pad_maximum_fusion.5.edges_ref
  81.4 0.0 collective-permute-done.6.near_ref
  81.4 5.9 %collective-permute-done.7.far_ref = bf16[6,80,512]{2,1,0:T(8,128)(2,1)S(1)} collective-permute-done((bf16[6,80,512]{2,1,0:T(8,128)(2,1)S(1)}, bf16[6,80,512]{2,1,0:T(8,128)(2,1)S(1)}, u32[]{:S(2)}, u32[]{:S(2)}) %collective-permute-start.7) | collective-permute-done | bytes 491552 | tf_op jit(solution)/shard_map/ppermute | solution.py:292
  87.3 0.8 copy-done.1
  88.1 34.0 %section_two.1 = bf16[8,64,512]{2,1,0:T(8,128)(2,1)} custom-call(s32[2]{0:T(128)} %pad_add_fusion.place_ref, s32[8,4]{1,0:T(8,128)} %copy.19.marks_ref, bf16[8,64,512]{2,1,0:T(8,128)(2,1)} %section_one.1.z_ref, bf16[8,16,512]{2,1,0:T(8,128)(2,1)} %pad_maximum_fusion.5.edges_ref, bf16[6,80,512]{2,1,0:T(8,128)(2,1)} %copy-done, bf16[6,80,512]{2,1,0:T(8,128)(2,1)} %copy-done.1, ...), custom_call_target="tpu_custom_call" | custom-call | tf_op jit(solution)/shard_map/section_two/pallas_call | solution.py:308
  (15 shorter events, 0.1 us)
Async XLA Ops:
  0.9 6.2 %collective-permute-start = (bf16[16,8,256]{2,1,0:T(8,128)(2,1)S(1)}, bf16[16,8,256]{2,1,0:T(8,128)(2,1)S(1)}, u32[]{:S(2)}, u32[]{:S(2)}) collective-permute-start(bf16[16,8,256]{2,1,0:T(8,128)(2,1)S(1)} %get-tuple-element.7), channel_id=1, source_target_pairs={{1,2},{2,1},{5,6},{6,5},{9,10},{10,9},{13,14},{14,13},{17,18},{18,... | collective-permute-start | bytes 196616 | tf_op jit(solution)/shard_map/ppermute | solution.py:292
  3.3 4.4 %collective-permute-start.1 = (bf16[16,8,256]{2,1,0:T(8,128)(2,1)S(1)}, bf16[16,8,256]{2,1,0:T(8,128)(2,1)S(1)}, u32[]{:S(2)}, u32[]{:S(2)}) collective-permute-start(bf16[16,8,256]{2,1,0:T(8,128)(2,1)S(1)} %get-tuple-element.8), channel_id=1, source_target_pairs={{0,1},{1,0},{2,3},{3,2},{4,5},{5,4},{6,7},{7,6},{8,9},{9,8},{10,11... | collective-permute-start | bytes 196616 | tf_op jit(solution)/shard_map/ppermute | solution.py:291
  7.8 10.9 %collective-permute-start.2 = (bf16[6,144,256]{2,1,0:T(8,128)(2,1)S(1)}, bf16[6,144,256]{2,1,0:T(8,128)(2,1)S(1)}, u32[]{:S(2)}, u32[]{:S(2)}) collective-permute-start(bf16[6,144,256]{2,1,0:T(8,128)(2,1)S(1)} %get-tuple-element.12), channel_id=1, source_target_pairs={{0,4},{4,0},{8,12},{12,8},{16,20},{20,16},{24,28},{28,24},{32,36},... | collective-permute-start | bytes 1327112 | tf_op jit(solution)/shard_map/ppermute | solution.py:291
  7.9 14.1 %collective-permute-start.3 = (bf16[6,144,256]{2,1,0:T(8,128)(2,1)S(1)}, bf16[6,144,256]{2,1,0:T(8,128)(2,1)S(1)}, u32[]{:S(2)}, u32[]{:S(2)}) collective-permute-start(bf16[6,144,256]{2,1,0:T(8,128)(2,1)S(1)} %get-tuple-element.11), channel_id=1, source_target_pairs={{4,8},{8,4},{12,16},{16,12},{20,24},{24,20},{28,32},{32,28},{36,40... | collective-permute-start | bytes 1327112 | tf_op jit(solution)/shard_map/ppermute | solution.py:292
  18.7 60.6 %copy-start.4 = (bf16[2,49,512]{2,0,1:T(2,128)(2,1)S(1)}, bf16[2,49,512]{2,0,1:T(2,128)(2,1)}, u32[]{:S(2)}) copy-start(bf16[2,49,512]{2,0,1:T(2,128)(2,1)} %param.22) | copy-start | bytes 301060
  18.7 61.3 %copy-start.5 = (s32[8,4]{0,1:T(4,128)S(1)}, s32[8,4]{0,1:T(4,128)}, u32[]{:S(2)}) copy-start(s32[8,4]{0,1:T(4,128)} %param.25) | copy-start | bytes 388
  18.7 3.3 %copy-start.2 = (bf16[6,144,256]{2,1,0:T(8,128)(2,1)}, bf16[6,144,256]{2,1,0:T(8,128)(2,1)S(1)}, u32[]{:S(2)}) copy-start(bf16[6,144,256]{2,1,0:T(8,128)(2,1)S(1)} %collective-permute-done.2.near_ref) | copy-start | bytes 1327108
  22.0 0.8 copy-start.3
  66.8 6.2 %collective-permute-start.4 = (bf16[8,8,512]{2,1,0:T(8,128)(2,1)S(1)}, bf16[8,8,512]{2,1,0:T(8,128)(2,1)S(1)}, u32[]{:S(2)}, u32[]{:S(2)}) collective-permute-start(bf16[8,8,512]{2,1,0:T(8,128)(2,1)S(1)} %get-tuple-element.15), channel_id=1, source_target_pairs={{1,2},{2,1},{5,6},{6,5},{9,10},{10,9},{13,14},{14,13},{17,18},{18,... | collective-permute-start | bytes 196616 | tf_op jit(solution)/shard_map/ppermute | solution.py:292
  70.3 4.4 %collective-permute-start.5 = (bf16[8,8,512]{2,1,0:T(8,128)(2,1)S(1)}, bf16[8,8,512]{2,1,0:T(8,128)(2,1)S(1)}, u32[]{:S(2)}, u32[]{:S(2)}) collective-permute-start(bf16[8,8,512]{2,1,0:T(8,128)(2,1)S(1)} %get-tuple-element.16), channel_id=1, source_target_pairs={{0,1},{1,0},{2,3},{3,2},{4,5},{5,4},{6,7},{7,6},{8,9},{9,8},{10,11... | collective-permute-start | bytes 196616 | tf_op jit(solution)/shard_map/ppermute | solution.py:291
  74.9 6.5 %collective-permute-start.6 = (bf16[6,80,512]{2,1,0:T(8,128)(2,1)S(1)}, bf16[6,80,512]{2,1,0:T(8,128)(2,1)S(1)}, u32[]{:S(2)}, u32[]{:S(2)}) collective-permute-start(bf16[6,80,512]{2,1,0:T(8,128)(2,1)S(1)} %get-tuple-element.10), channel_id=1, source_target_pairs={{0,4},{4,0},{8,12},{12,8},{16,20},{20,16},{24,28},{28,24},{32,36},... | collective-permute-start | bytes 1474568 | tf_op jit(solution)/shard_map/ppermute | solution.py:291
  75.0 12.3 %collective-permute-start.7 = (bf16[6,80,512]{2,1,0:T(8,128)(2,1)S(1)}, bf16[6,80,512]{2,1,0:T(8,128)(2,1)S(1)}, u32[]{:S(2)}, u32[]{:S(2)}) collective-permute-start(bf16[6,80,512]{2,1,0:T(8,128)(2,1)S(1)} %get-tuple-element.9), channel_id=1, source_target_pairs={{4,8},{8,4},{12,16},{16,12},{20,24},{24,20},{28,32},{32,28},{36,40... | collective-permute-start | bytes 1474568 | tf_op jit(solution)/shard_map/ppermute | solution.py:292
  81.4 5.9 %copy-start = (bf16[6,80,512]{2,1,0:T(8,128)(2,1)}, bf16[6,80,512]{2,1,0:T(8,128)(2,1)S(1)}, u32[]{:S(2)}) copy-start(bf16[6,80,512]{2,1,0:T(8,128)(2,1)S(1)} %collective-permute-done.6.near_ref) | copy-start | bytes 1474564
  87.3 0.8 copy-start.1
